TPU v7x, 512 devices: a whole 4x8x8 slice. The times are simulated.
512 devices in a mesh: space: 32 (over z_hi, x, core), chan: 16 (over z_lo, y).
Axes of the slice: x: 4, y: 8, z: 8 (z_hi: 4, z_lo: 2; z = z_hi * 2 + z_lo), core: 2. Of those that a mesh axis runs over, the one named last changes fastest.
Arguments:
- volume: bfloat16 [128, 128, 16, 128], P('chan', 'space'), may hold values from -6 to 6
- kernel: bfloat16 [128, 3, 3, 3, 128], P('chan'), may hold values from -0.109375 to 0.109375
- upstream: bfloat16 [128, 32, 4, 32], P('chan', 'space'), may hold values from -24 to 24
Outputs:
- pooled: bfloat16 [128, 32, 4, 32], P('chan', 'space')
- volume_grad: bfloat16 [128, 128, 16, 128], P('chan', 'space')
- kernel_grad: float32 [128, 3, 3, 3, 128], P('chan')
All inputs are finite; a program needn't handle non-finite values.
Results may differ from a plain program's by a relative error of at most 0.013.
Values may be sent and summed in bfloat16 or wider, within the bound.
A program may use at most 64 MiB of HBM per device.

v0:
```python
import jax
import jax.numpy as jnp
from jax import lax
from jax.sharding import PartitionSpec as P

slope_neg = 0.3
tap_table = ((1, 0, 0), (2, 1, 0), (0, 1, 1))


def from_behind(block, axis, distance):
    devices = range(lax.axis_size(axis))
    route = [(i - distance, i) for i in devices if i - distance in devices]
    return lax.ppermute(block, axis, route)


def strided_conv(operand, filters):
    return lax.conv_general_dilated(
        operand[None],
        filters,
        (2, 2, 2),
        ((0, 0), (1, 1), (1, 1)),
        dimension_numbers=("NCDHW", "IDHWO", "NCDHW"),
        preferred_element_type=jnp.float32,
    )[0]


def on_device(volume, kernel, upstream):
    in_block = volume.shape[0]
    out_block = upstream.shape[0]
    out_depth = volume.shape[1] // 2
    out_rows = volume.shape[2] // 2
    out_cols = volume.shape[3] // 2
    lower_rim = from_behind(volume[:, -1:], "space", 1)
    padded = jnp.concatenate([lower_rim, volume], axis=1)
    own_first = lax.axis_index("chan") * out_block
    empty = jnp.zeros((out_block, out_depth, out_rows, out_cols), jnp.float32)
    columns = lax.dynamic_slice_in_dim(
        lax.all_gather(kernel, "chan", axis=0, tiled=True), own_first, out_block, 4
    )
    pre = empty + strided_conv(lax.all_gather(padded, "chan", axis=0, tiled=True), columns)
    activated = jnp.where(pre > 0, pre, slope_neg * pre)
    block_shape = (out_block, out_depth // 2, 2, out_rows // 2, 2, out_cols // 2, 2)
    pooled = jnp.mean(activated.reshape(block_shape), axis=(2, 4, 6)).astype(jnp.bfloat16)
    spread = upstream.astype(jnp.float32) * 0.125
    spread = jnp.broadcast_to(spread[:, :, None, :, None, :, None], block_shape).reshape(pre.shape)
    pre_grad = (spread * jnp.where(pre > 0, 1.0, slope_neg)).astype(jnp.bfloat16)
    upper_rim = from_behind(pre_grad[:, :1], "space", -1)
    extended = jnp.concatenate([pre_grad, upper_rim], axis=1)
    panel = lax.all_gather(extended, "chan", axis=0, tiled=True)
    offset = jnp.int32(0)
    phase_grad = jnp.zeros((2, 2, 2, in_block, out_depth, out_rows, out_cols), jnp.float32)
    weight_grad = jnp.zeros((in_block, 3, 3, 3, kernel.shape[4]), jnp.float32)
    columns = lax.dynamic_slice_in_dim(kernel, offset, panel.shape[0], 4)
    grad_pad = jnp.pad(panel, ((0, 0), (0, 0), (0, 1), (0, 1)))
    phase_sums = {}
    for depth_tap, depth_par, depth_off in tap_table:
        for row_tap, row_par, row_off in tap_table:
            for col_tap, col_par, col_off in tap_table:
                shifted = grad_pad[
                    :,
                    depth_off : depth_off + out_depth,
                    row_off : row_off + out_rows,
                    col_off : col_off + out_cols,
                ]
                term = jnp.einsum(
                    "co,ozyx->czyx",
                    columns[:, depth_tap, row_tap, col_tap, :],
                    shifted,
                    preferred_element_type=jnp.float32,
                )
                phase_key = (depth_par, row_par, col_par)
                if phase_key in phase_sums:
                    phase_sums[phase_key] = phase_sums[phase_key] + term
                else:
                    phase_sums[phase_key] = term
    stacked = jnp.stack(
        [
            phase_sums[first, second, third]
            for first in (0, 1)
            for second in (0, 1)
            for third in (0, 1)
        ]
    )
    phase_grad = stacked.reshape(phase_grad.shape)
    weight_part = lax.conv_general_dilated(
        padded[None],
        panel[:, :out_depth][None],
        (1, 1, 1),
        ((0, 0), (1, 0), (1, 0)),
        rhs_dilation=(2, 2, 2),
        dimension_numbers=("CNDHW", "IODHW", "NDHWC"),
        preferred_element_type=jnp.float32,
    )
    weight_grad = lax.dynamic_update_slice_in_dim(weight_grad, weight_part, offset, 4)
    phase_grad, weight_grad = (phase_grad, weight_grad)
    input_grad = phase_grad.transpose(3, 4, 0, 5, 1, 6, 2).reshape(volume.shape)
    kernel_grad = lax.psum(weight_grad, "space")
    return (pooled, input_grad.astype(jnp.bfloat16), kernel_grad)


def solution(mesh):
    return jax.shard_map(
        on_device,
        mesh=mesh,
        in_specs=(
            P("chan", "space", None, None),
            P("chan", None, None, None, None),
            P("chan", "space", None, None),
        ),
        out_specs=(
            P("chan", "space", None, None),
            P("chan", "space", None, None),
            P("chan", None, None, None, None),
        ),
        check_vma=False,
    )
```

profile of v0, /device:TPU:1, one launch (start us, length us, event | category | flops | bytes accessed | tf_op | source)
XLA Modules:
  0.0 439.3 jit_solution(8369169473924084968)
XLA Ops:
  7.2 0.0 all-gather.2.cloned.1.call-start
  7.2 0.8 slice.133
  8.0 4.5 %collective-permute-start = (bf16[8,1,16,128]{3,2,1,0:T(8,128)(2,1)S(1)}, bf16[8,1,16,128]{3,2,1,0:T(8,128)(2,1)S(1)}, u32[]{:S(2)}, u32[]{:S(2)}) collective-permute-start(bf16[8,1,16,128]{3,2,1,0:T(8,128)(2,1)S(1)} %slice.133), channel_id=1, source_target_pairs={{0,16},{16,32},{32,48},{48,64},{64,80},{80,96},{96,112},{112,128},... | collective-permute-start | bytes 98312 | tf_op jit(solution)/shard_map/ppermute | solution.py:13
  12.5 4.3 collective-permute-done
  16.8 0.9 constant_dynamic-update-slice_fusion
  17.7 0.7 copy-done
  18.4 0.0 all-gather.2.cloned.1.call-update
  18.4 0.0 all-reduce.3.cloned.1.call-start
  18.5 0.7 multiply_bitcast_fusion
  19.2 0.1 copy.66
  19.2 0.1 broadcast_in_dim.29
  19.3 0.1 copy.67
  19.4 33.0 %all_gather.10 = bf16[128,3,3,3,128]{4,0,3,2,1:T(8,128)(2,1)S(1)} all-gather(bf16[8,3,3,3,128]{4,0,3,2,1:T(8,128)(2,1)} %param.4), channel_id=1, replica_groups=mesh['space'=32,'chan'=16] {'chan'}, dimensions={0}, use_global_device_ids=true | all-gather | bytes 940032 | tf_op jit(solution)/shard_map/all_gather | solution.py:38
  52.5 7.8 %copy.75 = bf16[1,8,5,16,128]{1,0,4,3,2:T(2,128)(2,1)} copy(bf16[1,8,5,16,128]{4,3,2,1,0:T(8,128)(2,1)} %bitcast.294) | data formatting | bytes 327680 | tf_op jit(solution)/shard_map/broadcast_in_dim | solution.py:86
  60.3 27.8 %all-gather.2.cloned.1.call-done = bf16[128,5,16,128]{3,2,1,0:T(8,128)(2,1)} async-done(((bf16[8,5,16,128]{3,2,1,0:T(8,128)(2,1)}), bf16[128,5,16,128]{3,2,1,0:T(8,128)(2,1)}) %all-gather.2.cloned.1.call-update) | async-done | bytes 2621456 | tf_op jit(solution)/shard_map/all_gather | solution.py:40
  88.1 4.6 %copy.60 = bf16[128,5,16,128]{0,2,3,1:T(8,128)(2,1)S(1)} copy(bf16[128,5,16,128]{3,2,1,0:T(8,128)(2,1)} %all-gather.2.cloned.1.call-done) | data formatting | bytes 5242880 | tf_op jit(solution)/shard_map/all_gather | solution.py:40
  92.8 0.5 pad.5
  93.3 1.1 copy.62
  94.4 0.1 slice.173
  94.5 2.3 compare_select_fusion
  96.9 0.8 copy.68
  97.7 0.2 reshape.45
  97.9 11.7 %collective-permute-start.1 = (bf16[8,1,8,64]{3,0,2,1:T(8,128)(2,1)S(1)}, bf16[8,1,8,64]{3,0,2,1:T(8,128)(2,1)S(1)}, u32[]{:S(2)}, u32[]{:S(2)}) collective-permute-start(bf16[8,1,8,64]{3,0,2,1:T(8,128)(2,1)S(1)} %slice.176), channel_id=1, source_target_pairs={{16,0},{32,16},{48,32},{64,48},{80,64},{96,80},{112,96},{128,112},... | collective-permute-start | bytes 24584 | tf_op jit(solution)/shard_map/ppermute | solution.py:13
  109.6 0.8 copy.64
  110.4 0.2 reshape.47
  110.7 0.1 copy.65
  110.8 0.2 reduce_sum.18
  111.0 0.7 copy.77
  111.7 1.1 collective-permute-done.1
  112.9 30.1 %all_gather.11 = bf16[128,3,8,64]{3,2,1,0:T(8,128)(2,1)S(1)} all-gather(bf16[8,3,8,64]{3,2,1,0:T(8,128)(2,1)S(1)} %pad_maximum_fusion), channel_id=1, replica_groups=mesh['space'=32,'chan'=16] {'chan'}, dimensions={0}, use_global_device_ids=true | all-gather | bytes 417792 | tf_op jit(solution)/shard_map/all_gather | solution.py:49
  143.0 0.5 copy.71
  143.5 0.3 fusion.81
  143.8 0.3 fusion.69
  144.0 0.3 fusion.62
  144.3 0.3 fusion.83
  144.6 0.3 fusion.74
  145.0 0.3 fusion.64
  145.3 0.3 fusion.52
  145.6 0.3 fusion.50
  145.9 0.3 fusion.48
  146.2 0.3 fusion.86
  146.5 0.3 fusion.49
  146.8 0.3 fusion.51
  147.1 0.3 fusion.53
  147.4 0.3 fusion.47
  147.7 0.3 fusion.78
  148.0 0.3 fusion.89
  148.3 0.3 fusion.29
  148.6 0.3 convolution_add_fusion.3
  148.9 0.3 convolution_add_fusion.5
  149.3 13.7 %fusion.45 = f32[8,3,3,3,128]{4,0,3,2,1:T(8,128)} fusion(bf16[1,8,5,16,128]{1,0,4,3,2:T(2,128)(2,1)} %copy.75, bf16[1,128,2,8,64]{1,4,3,2,0:T(8,128)(2,1)S(1)} %slice_bitcast_fusion), kind=kOutput, calls=%fused_computation.56 | convolution fusion | flops 53981184 | bytes 536576 | tf_op jit(solution)/shard_map/conv_general_dilated | solution.py:85
  162.9 0.0 all-reduce.3.cloned.1.call-update
  162.9 0.3 fusion.41
  163.2 0.3 fusion.39
  163.6 0.3 fusion.37
  163.9 0.3 fusion.35
  164.2 0.3 fusion.15
  164.6 0.3 fusion.33
  164.9 0.3 fusion.31
  165.2 0.3 fusion.43
  165.6 1.5 copy.74
  167.0 1.5 copy.78
  168.5 262.4 %all-reduce.3.cloned.1.call-done = f32[8,3,3,3,128]{4,0,3,2,1:T(8,128)} async-done(((f32[8,3,3,3,128]{4,0,3,2,1:T(8,128)}), f32[8,3,3,3,128]{4,0,3,2,1:T(8,128)}) %all-reduce.3.cloned.1.call-update) | async-done | bytes 110608 | tf_op jit(solution)/shard_map/psum | solution.py:97
  430.9 1.5 copy.118
  (14 shorter events, 0.1 us)
Async XLA Ops:
  7.2 81.0 %all-gather.2.cloned.1.call-start = ((), (), s32[]{:S(2)}) async-start(), calls=%async_computation | async-start | bytes 2785280 | tf_op jit(solution)/shard_map/all_gather | solution.py:40
  8.0 8.8 %collective-permute-start = (bf16[8,1,16,128]{3,2,1,0:T(8,128)(2,1)S(1)}, bf16[8,1,16,128]{3,2,1,0:T(8,128)(2,1)S(1)}, u32[]{:S(2)}, u32[]{:S(2)}) collective-permute-start(bf16[8,1,16,128]{3,2,1,0:T(8,128)(2,1)S(1)} %slice.133), channel_id=1, source_target_pairs={{0,16},{16,32},{32,48},{48,64},{64,80},{80,96},{96,112},{112,128},... | collective-permute-start | bytes 98312 | tf_op jit(solution)/shard_map/ppermute | solution.py:13
  17.7 0.7 copy-start
  18.4 412.5 %all-reduce.3.cloned.1.call-start = ((), (), s32[]{:S(2)}) async-start(), calls=%async_computation.1 | async-start | bytes 221184 | tf_op jit(solution)/shard_map/psum | solution.py:97
  93.3 1.3 copy-start.2
  96.8 46.6 %copy-start.1 = (bf16[8,3,3,3,128]{4,0,3,2,1:T(8,128)(2,1)S(1)}, bf16[8,3,3,3,128]{4,0,3,2,1:T(8,128)(2,1)}, u32[]{:S(2)}) copy-start(bf16[8,3,3,3,128]{4,0,3,2,1:T(8,128)(2,1)} %param.4) | copy-start | bytes 165892
  97.9 15.0 %collective-permute-start.1 = (bf16[8,1,8,64]{3,0,2,1:T(8,128)(2,1)S(1)}, bf16[8,1,8,64]{3,0,2,1:T(8,128)(2,1)S(1)}, u32[]{:S(2)}, u32[]{:S(2)}) collective-permute-start(bf16[8,1,8,64]{3,0,2,1:T(8,128)(2,1)S(1)} %slice.176), channel_id=1, source_target_pairs={{16,0},{32,16},{48,32},{64,48},{80,64},{96,80},{112,96},{128,112},... | collective-permute-start | bytes 24584 | tf_op jit(solution)/shard_map/ppermute | solution.py:13
Sparse Core Ops, SparseCore 0:
  18.5 69.5 all-gather.1
  163.1 267.7 all-reduce.2
where the time goes:
time: 440 us; the launch traced here: 439 us
  waiting for transfers between devices  296 us (67%)
  blocking collectives  63.1 us (14%)
  local copies, waits for them, and re-layouts  24.7 us (6%)
  matrix products  24.3 us (6%)
  starting transfers between devices  16.3 us (4%)
  between operations  14.3 us (3%)
    psum x1, waiting for transfers between devices, on_device(): kernel_grad = lax.psum(weight_grad, 'space')  262 us
    all_gather x1, blocking collectives, on_device(): lax.all_gather(kernel, 'chan', axis=0, tiled=True)  33 us
    all_gather x1, blocking collectives, on_device(): panel = lax.all_gather(extended, 'chan', axis=0, tiled=True)  30.1 us
    all_gather x1, waiting for transfers between devices, on_device(): lax.all_gather(padded, 'chan', axis=0, tiled=True)  27.8 us
    ppermute x2, starting transfers between devices, from_behind(): return lax.ppermute(block, axis, route)  16.2 us
    conv_general_dilated x1, matrix products, on_device(): lax.conv_general_dilated(padded[None], panel[:, :out_depth][None], (1, 1,...  13.7 us
  transfers between devices with their start and end apart: 4, of which 4 were waited for; matrix products, arithmetic and copies ran while one was open for 4% of the time, Pallas kernels for 0%

commit v1 on v0

v1 whole, which is shorter than its diff:
```python
import jax
import jax.numpy as jnp
from jax import lax
from jax.experimental import pallas as pl
from jax.experimental.pallas import tpu as pltpu
from jax.sharding import PartitionSpec as P

slope_neg = 0.3
MESH = pl.DeviceIdType.MESH
bf16, f32, i32 = jnp.bfloat16, jnp.float32, jnp.int32


def iota(shape, dim):
    return lax.broadcasted_iota(i32, shape, dim)


def one_hot(condition):
    return jnp.where(condition, 1.0, 0.0).astype(bf16)


def row_picker():
    out, inn = iota((160, 128), 0), iota((160, 128), 1)
    same = (out & 7) == (inn >> 4)
    return one_hot(same & ((inn & 15) == 4 * ((out >> 3) & 3) + (out >> 5) - 1))


def column_picker():
    inn, out = iota((256, 384), 0), iota((256, 384), 1)
    same = (inn >> 7) == ((out >> 6) & 1)
    return one_hot(same & ((inn & 127) == 2 * (out & 63) + (out >> 7) - 1))


def pool_picker():
    coarse, fine = iota((128, 1024), 0), iota((128, 1024), 1)
    return one_hot(
        ((coarse >> 5) == ((fine >> 7) & 3)) & ((coarse & 31) == ((fine >> 1) & 31))
    )


def channel_first():
    out, inn = iota((128, 128), 0), iota((128, 128), 1)
    return one_hot(((out >> 4) == (inn & 7)) & ((out & 15) == (inn >> 3)))


def front_kernel(vol, rim, weights, up, part, taps, spread, stage):
    pick_rows = row_picker()
    pick_cols = column_picker()
    planes = []
    for p in range(5):
        plane = rim[:, 0] if p == 0 else vol[:, p - 1]
        rows = jnp.dot(pick_rows, plane.reshape(128, 128), preferred_element_type=f32)
        planes.append(rows.astype(bf16))
    for b in range(3):
        pairs = jnp.concatenate(
            [
                jnp.concatenate(
                    [u[32 * b : 32 * b + 32], u[32 * b + 64 : 32 * b + 96]], axis=1
                )
                for u in planes
            ],
            axis=0,
        )
        picked = jnp.dot(pairs, pick_cols, preferred_element_type=f32)
        for e in range(3):
            for a in range(3):
                for z in range(2):
                    for yh in range(4):
                        src = ((2 * z + a) * 4 + yh) * 8
                        dst = ((b * 3 + e) * 3 + a) * 8
                        lane = (z * 4 + yh) * 128
                        stage[dst : dst + 8, lane : lane + 128] = picked[
                            src : src + 8, e * 128 : e * 128 + 128
                        ]
    columns = stage[...].astype(bf16)
    taps[...] = columns
    part[...] = lax.dot_general(
        weights[...], columns, (((0,), (0,)), ((), ())), preferred_element_type=f32
    ).reshape(16, 8, 1024)
    spread[...] = jnp.dot(up[...], pool_picker(), preferred_element_type=f32) * 0.125


def everyone(axis, n):
    me = lax.axis_index(axis)
    barrier = pltpu.get_barrier_semaphore()
    for k in range(1, n):
        pl.semaphore_signal(
            barrier, inc=1, device_id={axis: lax.rem(me + k, n)}, device_id_type=MESH
        )
    pl.semaphore_wait(barrier, n - 1)
    return me


def chan_kernel(n, part, spread, pre_out, panel_out, got, panel, s1, r1, s2, r2):
    me = everyone("chan", n)
    copies = []
    for k in range(1, n):
        peer = lax.rem(me + k, n)
        copy = pltpu.make_async_remote_copy(
            src_ref=part.at[peer],
            dst_ref=got.at[k],
            send_sem=s1.at[k],
            recv_sem=r1.at[k],
            device_id={"chan": peer},
            device_id_type=MESH,
        )
        copy.start()
        copies.append(copy)
    pre = part[me]
    for k in range(1, n):
        copies[k - 1].wait_recv()
        pre = pre + got[k]
    pre_out[...] = pre
    grad = (spread[...] * jnp.where(pre > 0, 1.0, slope_neg)).astype(bf16)
    panel[me] = grad
    gathers = []
    for k in range(1, n):
        copy = pltpu.make_async_remote_copy(
            src_ref=panel.at[me],
            dst_ref=panel.at[me],
            send_sem=s2.at[k],
            recv_sem=r2.at[k],
            device_id={"chan": lax.rem(me + k, n)},
            device_id_type=MESH,
        )
        copy.start()
        gathers.append(copy)
    for copy in copies:
        copy.wait_send()
    for copy in gathers:
        copy.wait_recv()
    panel_out[...] = panel[...]
    for copy in gathers:
        copy.wait_send()


def weight_kernel(taps, panel, out):
    grads = panel[...].reshape(128, 1024)
    total = lax.dot_general(
        taps[...], grads, (((1,), (1,)), ((), ())), preferred_element_type=f32
    )
    out[0:27] = total.reshape(27, 8, 128)
    out[27:32] = jnp.zeros((5, 8, 128), f32)


def volume_kernel(weights, panel, rim, pre, out, pooled, terms, rows, fold):
    pick_cols = column_picker()
    w = weights[...]
    terms[:, 0:1024] = jnp.dot(w, panel[...].reshape(128, 1024), preferred_element_type=f32)
    terms[:, 1024:1536] = jnp.dot(w, rim[...].reshape(128, 512), preferred_element_type=f32)
    for b in range(3):
        for a in range(3):
            for zi in range(2):
                z = zi + 1 if a == 0 else zi
                for yh in range(4):
                    dst = (((b * 3 + a) * 2 + zi) * 4 + yh) * 8
                    lane = (z * 4 + yh) * 128
                    for e in range(3):
                        src = ((b * 3 + e) * 3 + a) * 8
                        rows[dst : dst + 8, e * 128 : e * 128 + 128] = terms[
                            src : src + 8, lane : lane + 128
                        ]
    high = rows[...].astype(bf16)
    low = (rows[...] - high.astype(f32)).astype(bf16)
    dims = (((1,), (1,)), ((), ()))
    fold[...] = lax.dot_general(high, pick_cols, dims, preferred_element_type=f32)
    fold[...] += lax.dot_general(low, pick_cols, dims, preferred_element_type=f32)
    order = channel_first()
    depth_terms = (((1, 0),), ((2, 0), (0, 0)), ((1, 1),), ((2, 1), (0, 1)))
    for i in range(4):
        sums = []
        for j in range(16):
            if j % 2 == 0:
                row_terms = ((1, j // 2),)
            elif j < 15:
                row_terms = ((2, j // 2), (0, j // 2 + 1))
            else:
                row_terms = ((2, j // 2),)
            acc = None
            for a, zi in depth_terms[i]:
                for b, y in row_terms:
                    src = (((b * 3 + a) * 2 + zi) * 4 + y // 2) * 8
                    lane = (y % 2) * 128
                    term = fold[src : src + 8, lane : lane + 128]
                    acc = term if acc is None else acc + term
            sums.append(acc)
        plane = jnp.concatenate(sums, axis=0).astype(bf16)
        moved = jnp.dot(order, plane, preferred_element_type=f32).astype(bf16)
        out[:, i] = moved.reshape(8, 16, 128)
    act = jnp.where(pre[...] > 0, pre[...], slope_neg * pre[...])
    first = act.astype(bf16)
    rest = act - first.astype(f32)
    second = rest.astype(bf16)
    third = (rest - second.astype(f32)).astype(bf16)
    pick = pool_picker()
    total = sum(
        lax.dot_general(piece, pick, dims, preferred_element_type=f32)
        for piece in (third, second, first)
    )
    pooled[...] = (total * 0.125).astype(bf16)


def space_kernel(n, terms, out, got, mine, s1, r1, s2, r2):
    me = everyone("space", n)
    copies = []
    for k in range(1, n):
        peer = lax.rem(me + k, n)
        copy = pltpu.make_async_remote_copy(
            src_ref=terms.at[peer],
            dst_ref=got.at[k],
            send_sem=s1.at[k],
            recv_sem=r1.at[k],
            device_id={"space": peer},
            device_id_type=MESH,
        )
        copy.start()
        copies.append(copy)
    total = terms[me]
    for k in range(1, n):
        copies[k - 1].wait_recv()
        total = total + got[k]
    mine[me] = total
    gathers = []
    for k in range(1, n):
        copy = pltpu.make_async_remote_copy(
            src_ref=mine.at[me],
            dst_ref=mine.at[me],
            send_sem=s2.at[k],
            recv_sem=r2.at[k],
            device_id={"space": lax.rem(me + k, n)},
            device_id_type=MESH,
        )
        copy.start()
        gathers.append(copy)
    for copy in copies:
        copy.wait_send()
    for copy in gathers:
        copy.wait_recv()
    out[...] = mine[...]
    for copy in gathers:
        copy.wait_send()


def in_vmem(count):
    return [pl.BlockSpec(memory_space=pltpu.VMEM)] * count


def shaped(*shape, dtype=f32):
    return jax.ShapeDtypeStruct(shape, dtype)


def front(vol, rim, weights, up):
    return pl.pallas_call(
        front_kernel,
        out_shape=(
            shaped(16, 8, 1024),
            shaped(216, 1024, dtype=bf16),
            shaped(8, 1024),
        ),
        in_specs=in_vmem(4),
        out_specs=tuple(in_vmem(3)),
        scratch_shapes=[pltpu.VMEM((216, 1024), f32)],
        cost_estimate=pl.CostEstimate(flops=200_000_000, bytes_accessed=1_500_000, transcendentals=0),
    )(vol, rim, weights, up)


def chan_exchange(part, spread):
    n = lax.axis_size("chan")
    sem = pltpu.SemaphoreType.DMA((n,))
    return pl.pallas_call(
        lambda *refs: chan_kernel(n, *refs),
        name="chan_exchange",
        out_shape=(shaped(8, 1024), shaped(n, 8, 1024, dtype=bf16)),
        in_specs=in_vmem(2),
        out_specs=tuple(in_vmem(2)),
        scratch_shapes=[
            pltpu.VMEM((n, 8, 1024), f32),
            pltpu.VMEM((n, 8, 1024), bf16),
            sem,
            sem,
            sem,
            sem,
        ],
        compiler_params=pltpu.CompilerParams(collective_id=0, has_side_effects=True),
    )(part, spread)


def weight_grad(taps, panel):
    return pl.pallas_call(
        weight_kernel,
        out_shape=shaped(32, 8, 128),
        in_specs=in_vmem(2),
        out_specs=in_vmem(1)[0],
        cost_estimate=pl.CostEstimate(flops=200_000_000, bytes_accessed=1_500_000, transcendentals=0),
    )(taps, panel)


def volume_grad(weights, panel, rim, pre):
    return pl.pallas_call(
        volume_kernel,
        out_shape=(shaped(8, 4, 16, 128, dtype=bf16), shaped(8, 128, dtype=bf16)),
        in_specs=in_vmem(4),
        out_specs=tuple(in_vmem(2)),
        scratch_shapes=[
            pltpu.VMEM((216, 1536), f32),
            pltpu.VMEM((576, 384), f32),
            pltpu.VMEM((576, 256), f32),
        ],
        cost_estimate=pl.CostEstimate(flops=400_000_000, bytes_accessed=3_000_000, transcendentals=0),
    )(weights, panel, rim, pre)


def space_sum(terms):
    n = lax.axis_size("space")
    sem = pltpu.SemaphoreType.DMA((n,))
    return pl.pallas_call(
        lambda *refs: space_kernel(n, *refs),
        name="space_sum",
        out_shape=shaped(n, 8, 128),
        in_specs=in_vmem(1),
        out_specs=in_vmem(1)[0],
        scratch_shapes=[
            pltpu.VMEM((n, 8, 128), f32),
            pltpu.VMEM((n, 8, 128), f32),
            sem,
            sem,
            sem,
            sem,
        ],
        compiler_params=pltpu.CompilerParams(collective_id=1, has_side_effects=True),
    )(terms)


def from_behind(block, axis, distance):
    devices = range(lax.axis_size(axis))
    route = [(i - distance, i) for i in devices if i - distance in devices]
    return lax.ppermute(block, axis, route)


def on_device(volume, kernel, upstream):
    lower_rim = from_behind(volume[:, -1:], "space", 1)
    weights = kernel.transpose(2, 3, 1, 0, 4).reshape(216, 128)
    part, taps, spread = front(volume, lower_rim, weights, upstream.reshape(8, 128))
    pre, panel = chan_exchange(part, spread)
    upper_rim = from_behind(panel[:, :, :512], "space", -1)
    terms = weight_grad(taps, panel)
    input_grad, pooled = volume_grad(weights, panel, upper_rim, pre)
    total = space_sum(terms)
    kernel_grad = total[:27].reshape(3, 3, 3, 8, 128).transpose(3, 2, 0, 1, 4)
    return pooled.reshape(upstream.shape), input_grad, kernel_grad


def solution(mesh):
    return jax.shard_map(
        on_device,
        mesh=mesh,
        in_specs=(
            P("chan", "space", None, None),
            P("chan", None, None, None, None),
            P("chan", "space", None, None),
        ),
        out_specs=(
            P("chan", "space", None, None),
            P("chan", "space", None, None),
            P("chan", None, None, None, None),
        ),
        check_vma=False,
    )
```

time: 440 us -> 84.1 us (0.19)
  waiting for transfers between devices: 296 us -> 3.01 us
  Pallas kernels: 0 us -> 65.4 us
  blocking collectives: 63.1 us -> 0 us
  matrix products: 24.3 us -> 0 us
  local copies, waits for them, and re-layouts: 24.7 us -> 7.15 us
  between operations: 14.3 us -> 0.7 us
  starting transfers between devices: 16.3 us -> 7.48 us
    psum x1 -> x0, waiting for transfers between devices: 262 us -> none  [on_device(): kernel_grad = lax.psum(weight_grad, 'space')]
    pallas_call x0 -> x5, Pallas kernels: none -> 65.4 us  [the longest x1 30 us: space_sum(): pl.pallas_call(lambda *refs: space_kernel(n, *refs), name='space_sum', ou...]
    all_gather x2 -> x0, blocking collectives: 63.1 us -> none  [the longest x1 33 us: on_device(): lax.all_gather(kernel, 'chan', axis=0, tiled=True)]
    all_gather x1 -> x0, waiting for transfers between devices: 27.8 us -> none  [on_device(): lax.all_gather(padded, 'chan', axis=0, tiled=True)]
    conv_general_dilated x2 -> x0, matrix products: 16 us -> none  [the longest x1 13.7 us: on_device(): lax.conv_general_dilated(padded[None], panel[:, :out_depth][None], (1, 1,...]
    ppermute x2, starting transfers between devices: 16.2 us -> 7.48 us  [from_behind(): return lax.ppermute(block, axis, route)]
    broadcast_in_dim x6 -> x0, local copies, waits for them, and re-layouts: 8.62 us -> none  [the longest x1 7.83 us: on_device(): padded[None]]
    dot_general x27 -> x0, matrix products: 8.32 us -> none  [on_device(): jnp.einsum('co,ozyx->czyx', columns[:, depth_tap, row_tap, col_tap, :], s...]
  transfers between devices with their start and end apart: 4 -> 2, of which waited for: 4 -> 1; matrix products, arithmetic and copies ran while one was open for 4% -> 2% of each run, Pallas kernels for 0% -> 38%
where the time goes in v1:
time: 84.1 us; the launch traced here: 83.7 us
  Pallas kernels  65.4 us (78%)
  starting transfers between devices  7.48 us (9%)
  local copies, waits for them, and re-layouts  7.15 us (9%)
  waiting for transfers between devices  3.01 us (4%)
    pallas_call x1, Pallas kernels, space_sum(): pl.pallas_call(lambda *refs: space_kernel(n, *refs), name='space_sum', ou...  30 us
    pallas_call x1, Pallas kernels, chan_exchange(): pl.pallas_call(lambda *refs: chan_kernel(n, *refs), name='chan_exchange',...  27.9 us
    ppermute x2, starting transfers between devices, from_behind(): return lax.ppermute(block, axis, route)  7.48 us
    pallas_call x1, Pallas kernels, volume_grad(): pl.pallas_call(volume_kernel, out_shape=(shaped(8, 4, 16, 128, dtype=bf16...  3.11 us
    ppermute x2, waiting for transfers between devices, from_behind(): return lax.ppermute(block, axis, route)  3.01 us
    pallas_call x1, Pallas kernels, front(): pl.pallas_call(front_kernel, out_shape=(shaped(16, 8, 1024), shaped(216,...  2.38 us
    pallas_call x1, Pallas kernels, weight_grad(): pl.pallas_call(weight_kernel, out_shape=shaped(32, 8, 128), in_specs=in_v...  2.02 us
  transfers between devices with their start and end apart: 2, of which 1 were waited for; matrix products, arithmetic and copies ran while one was open for 2% of the time, Pallas kernels for 38%

profile of v1, /device:TPU:1, one launch (start us, length us, event | category | flops | bytes accessed | tf_op | source)
XLA Modules:
  0.0 83.7 jit_solution(16472291578501822289)
XLA Ops:
  0.6 0.0 copy-start.1
  0.6 0.0 copy-start
  0.7 0.8 slice.9
  1.4 4.5 %collective-permute-start = (bf16[8,1,16,128]{3,2,1,0:T(8,128)(2,1)S(1)}, bf16[8,1,16,128]{3,2,1,0:T(8,128)(2,1)S(1)}, u32[]{:S(2)}, u32[]{:S(2)}) collective-permute-start(bf16[8,1,16,128]{3,2,1,0:T(8,128)(2,1)S(1)} %slice.9), channel_id=1, source_target_pairs={{0,16},{16,32},{32,48},{48,64},{64,80},{80,96},{96,112},{112,128},... | collective-permute-start | bytes 98312 | tf_op jit(solution)/shard_map/ppermute | solution.py:336
  5.9 0.0 copy-done.1
  5.9 0.7 reshape.19.up
  6.6 0.0 copy-done
  6.6 0.6 copy.6
  7.2 3.0 %collective-permute-done.rim = bf16[8,1,16,128]{3,2,1,0:T(8,128)(2,1)S(1)} collective-permute-done((bf16[8,1,16,128]{3,2,1,0:T(8,128)(2,1)S(1)}, bf16[8,1,16,128]{3,2,1,0:T(8,128)(2,1)S(1)}, u32[]{:S(2)}, u32[]{:S(2)}) %collective-permute-start) | collective-permute-done | bytes 32800 | tf_op jit(solution)/shard_map/ppermute | solution.py:336
  10.2 0.0 copy-start.3
  10.2 0.6 copy-done.3
  10.9 2.4 %shard_map.58 = (f32[16,8,1024]{2,1,0:T(8,128)}, bf16[216,1024]{1,0:T(8,128)(2,1)}, f32[8,1024]{1,0:T(8,128)}) custom-call(bf16[8,4,16,128]{3,2,1,0:T(8,128)(2,1)} %vol.1, bf16[8,1,16,128]{3,2,1,0:T(8,128)(2,1)} %copy-done.3, bf16[216,128]{1,0:T(8,128)(2,1)} %bitcast.10, bf16[8,128]{1,0:T(8,128)(2,1)} %reshape.19.up), custom_call_target="tpu_custom_call" | custom-call | flops 200000000 | bytes 1500000 | tf_op jit(solution)/shard_map/pallas_call | solution.py:252
  13.2 27.9 %chan_exchange.1 = (f32[8,1024]{1,0:T(8,128)}, bf16[16,8,1024]{2,1,0:T(8,128)(2,1)}) custom-call(f32[16,8,1024]{2,1,0:T(8,128)} %get-tuple-element.10.refs_0_, f32[8,1024]{1,0:T(8,128)} %get-tuple-element.11.refs_1_), custom_call_target="tpu_custom_call" | custom-call | tf_op jit(solution)/shard_map/chan_exchange/pallas_call | solution.py:269
  41.2 0.9 %slice.10 = bf16[16,8,512]{2,1,0:T(8,128)(2,1)S(1)} slice(bf16[16,8,1024]{2,1,0:T(8,128)(2,1)} %get-tuple-element.12.panel), slice={[0:16], [0:8], [0:512]} | slice | bytes 262144 | tf_op jit(solution)/shard_map/slice | solution.py:344
  42.1 3.0 %collective-permute-start.1 = (bf16[16,8,512]{2,1,0:T(8,128)(2,1)S(1)}, bf16[16,8,512]{2,1,0:T(8,128)(2,1)S(1)}, u32[]{:S(2)}, u32[]{:S(2)}) collective-permute-start(bf16[16,8,512]{2,1,0:T(8,128)(2,1)S(1)} %slice.10), channel_id=1, source_target_pairs={{16,0},{32,16},{48,32},{64,48},{80,64},{96,80},{112,96},{128,112},... | collective-permute-start | bytes 393224 | tf_op jit(solution)/shard_map/ppermute | solution.py:336
  45.1 2.0 %shard_map.60.refs_0_ = f32[32,8,128]{2,1,0:T(8,128)} custom-call(bf16[216,1024]{1,0:T(8,128)(2,1)} %get-tuple-element.16.taps, bf16[16,8,1024]{2,1,0:T(8,128)(2,1)} %get-tuple-element.12.panel), custom_call_target="tpu_custom_call" | custom-call | flops 200000000 | bytes 1500000 | tf_op jit(solution)/shard_map/pallas_call | solution.py:288
  47.1 30.0 %space_sum.1 = f32[32,8,128]{2,1,0:T(8,128)} custom-call(f32[32,8,128]{2,1,0:T(8,128)} %shard_map.60.refs_0_), custom_call_target="tpu_custom_call" | custom-call | tf_op jit(solution)/shard_map/space_sum/pallas_call | solution.py:315
  77.1 0.0 slice-start
  77.1 0.9 %slice-done = f32[27,8,128]{2,1,0:T(8,128)S(1)} async-done(((f32[32,8,128]{2,1,0:T(8,128)}), f32[27,8,128]{2,1,0:T(8,128)S(1)}, s32[]{:S(2)}) %slice-start) | async-done | bytes 110616 | tf_op jit(solution)/shard_map/slice | solution.py:348
  78.0 0.7 copy.10
  78.6 0.0 collective-permute-done.1.rim
  78.6 0.0 copy-start.2
  78.6 0.6 copy-done.2
  79.3 3.1 %shard_map.59 = (bf16[8,4,16,128]{3,2,1,0:T(8,128)(2,1)}, bf16[8,128]{1,0:T(8,128)(2,1)}) custom-call(bf16[216,128]{1,0:T(8,128)(2,1)} %bitcast.11, bf16[16,8,1024]{2,1,0:T(8,128)(2,1)} %get-tuple-element.12.panel, bf16[16,8,512]{2,1,0:T(8,128)(2,1)} %copy-done.2, f32[8,1024]{1,0:T(8,128)} %get-tuple-element.13.pre), custom_call_target="tpu_custom_call" | custom-call | flops 400000000 | bytes 3000000 | tf_op jit(solution)/shard_map/pallas_call | solution.py:298
  82.4 1.4 %reshape.20 = bf16[8,1,4,32]{3,2,0,1:T(4,128)(2,1)} reshape(bf16[8,128]{1,0:T(8,128)(2,1)} %get-tuple-element.14) | data formatting | bytes 4096 | tf_op jit(solution)/shard_map/reshape | solution.py:349
Async XLA Ops:
  0.6 5.3 %copy-start.1 = (bf16[8,1,4,32]{3,2,1,0:T(4,128)(2,1)S(1)}, bf16[8,1,4,32]{3,2,1,0:T(4,128)(2,1)}, u32[]{:S(2)}) copy-start(bf16[8,1,4,32]{3,2,1,0:T(4,128)(2,1)} %param.5) | copy-start | bytes 6148
  0.6 6.0 %copy-start = (bf16[8,3,3,3,128]{4,0,3,2,1:T(8,128)(2,1)S(1)}, bf16[8,3,3,3,128]{4,0,3,2,1:T(8,128)(2,1)}, u32[]{:S(2)}) copy-start(bf16[8,3,3,3,128]{4,0,3,2,1:T(8,128)(2,1)} %param.4) | copy-start | bytes 165892
  1.4 8.8 %collective-permute-start = (bf16[8,1,16,128]{3,2,1,0:T(8,128)(2,1)S(1)}, bf16[8,1,16,128]{3,2,1,0:T(8,128)(2,1)S(1)}, u32[]{:S(2)}, u32[]{:S(2)}) collective-permute-start(bf16[8,1,16,128]{3,2,1,0:T(8,128)(2,1)S(1)} %slice.9), channel_id=1, source_target_pairs={{0,16},{16,32},{32,48},{48,64},{64,80},{80,96},{96,112},{112,128},... | collective-permute-start | bytes 98312 | tf_op jit(solution)/shard_map/ppermute | solution.py:336
  10.2 0.6 copy-start.3
  42.1 36.5 %collective-permute-start.1 = (bf16[16,8,512]{2,1,0:T(8,128)(2,1)S(1)}, bf16[16,8,512]{2,1,0:T(8,128)(2,1)S(1)}, u32[]{:S(2)}, u32[]{:S(2)}) collective-permute-start(bf16[16,8,512]{2,1,0:T(8,128)(2,1)S(1)} %slice.10), channel_id=1, source_target_pairs={{16,0},{32,16},{48,32},{64,48},{80,64},{96,80},{112,96},{128,112},... | collective-permute-start | bytes 393224 | tf_op jit(solution)/shard_map/ppermute | solution.py:336
  77.1 0.9 %slice-start = ((f32[32,8,128]{2,1,0:T(8,128)}), f32[27,8,128]{2,1,0:T(8,128)S(1)}, s32[]{:S(2)}) async-start(f32[32,8,128]{2,1,0:T(8,128)} %space_sum.1), calls=%async_computation | async-start | bytes 221184 | tf_op jit(solution)/shard_map/slice | solution.py:348
  78.6 0.6 copy-start.2

commit v2 on v0

v2 whole, which is shorter than its diff:
```python
import jax
import jax.numpy as jnp
from jax import lax
from jax.experimental import pallas as pl
from jax.experimental.pallas import tpu as pltpu
from jax.sharding import PartitionSpec as P

slope_neg = 0.3
MESH = pl.DeviceIdType.MESH
bf16, f32, i32 = jnp.bfloat16, jnp.float32, jnp.int32


def iota(shape, dim):
    return lax.broadcasted_iota(i32, shape, dim)


def one_hot(condition):
    return jnp.where(condition, 1.0, 0.0).astype(bf16)


def row_picker():
    out, inn = iota((160, 128), 0), iota((160, 128), 1)
    same = (out & 7) == (inn >> 4)
    return one_hot(same & ((inn & 15) == 4 * ((out >> 3) & 3) + (out >> 5) - 1))


def column_picker():
    inn, out = iota((256, 384), 0), iota((256, 384), 1)
    same = (inn >> 7) == ((out >> 6) & 1)
    return one_hot(same & ((inn & 127) == 2 * (out & 63) + (out >> 7) - 1))


def pool_picker():
    coarse, fine = iota((128, 1024), 0), iota((128, 1024), 1)
    return one_hot(
        ((coarse >> 5) == ((fine >> 7) & 3)) & ((coarse & 31) == ((fine >> 1) & 31))
    )


def channel_first():
    out, inn = iota((128, 128), 0), iota((128, 128), 1)
    row = 4 * ((inn >> 3) & 3) + (inn >> 5)
    return one_hot(((out >> 4) == (inn & 7)) & ((out & 15) == row))


def side_by_side(blocks):
    return jnp.concatenate(blocks, axis=1)


def block_kernel(
    n_space,
    vol,
    weights,
    up,
    pooled,
    grad_out,
    total_out,
    rim,
    stage,
    taps,
    part,
    from_z,
    z_sum,
    from_y,
    panel,
    rim_panel,
    folds,
    terms,
    got,
    mine,
    s_rim,
    r_rim,
    s_z,
    r_z,
    s_y,
    r_y,
    s_gy,
    r_gy,
    s_gz,
    r_gz,
    s_rs,
    r_rs,
    s_ag,
    r_ag,
):
    space, chan = lax.axis_index("space"), lax.axis_index("chan")
    half = lax.div(chan, 8)
    place = lax.rem(chan, 8)
    partner = lax.rem(chan + 8, 16)

    def along(k):
        return half * 8 + lax.rem(place + k, 8)

    def before(k):
        return half * 8 + lax.rem(place + 8 - k, 8)

    def ahead(k):
        return lax.rem(space + k, n_space)

    sent = []

    def send(src, dst, send_sem, recv_sem, **device):
        copy = pltpu.make_async_remote_copy(
            src_ref=src,
            dst_ref=dst,
            send_sem=send_sem,
            recv_sem=recv_sem,
            device_id=device,
            device_id_type=MESH,
        )
        copy.start()
        sent.append(copy)
        return copy

    barrier = pltpu.get_barrier_semaphore()
    for k in range(1, 8):
        pl.semaphore_signal(barrier, inc=1, device_id={"chan": along(k)}, device_id_type=MESH)
    pl.semaphore_signal(barrier, inc=1, device_id={"chan": partner}, device_id_type=MESH)
    for k in range(1, n_space):
        pl.semaphore_signal(barrier, inc=1, device_id={"space": ahead(k)}, device_id_type=MESH)

    pick_rows = row_picker()
    pick_cols = column_picker()

    def rows_of(plane):
        return jnp.dot(pick_rows, plane.reshape(128, 128), preferred_element_type=f32)

    planes = [None] + [rows_of(vol[:, p]).astype(bf16) for p in range(4)]
    pl.semaphore_wait(barrier, 8 + n_space - 1)
    rim_copy = send(vol.at[:, 3], rim, s_rim.at[0], r_rim.at[0], space=ahead(1))

    far_first = (4, 3, 5, 2, 6, 1, 7)
    w = weights[...]
    z_copies = {}
    for h in (1, 0):
        if h == 0:
            rim_copy.wait_recv()
            planes[0] = jnp.where(space > 0, rows_of(rim[...]), 0.0).astype(bf16)
        for b in range(3):
            pairs = jnp.concatenate(
                [
                    side_by_side([u[32 * b : 32 * b + 32], u[32 * b + 64 : 32 * b + 96]])
                    for u in planes[2 * h : 2 * h + 3]
                ],
                axis=0,
            )
            picked = jnp.dot(pairs, pick_cols, preferred_element_type=f32)
            for e in range(3):
                tap = b * 9 + e * 3
                stage[tap : tap + 3] = picked[:, e * 128 : e * 128 + 128].reshape(3, 4, 8, 128)
        columns = side_by_side([stage[:, q].reshape(216, 128) for q in range(4)]).astype(bf16)
        taps[h] = columns
        part[h] = lax.dot_general(
            w, columns, (((0,), (0,)), ((), ())), preferred_element_type=f32
        ).reshape(16, 8, 512)
        for k in far_first + (0,):
            other = (1 - half) * 8 + lax.rem(place + k, 8)
            z_copies[h, k] = send(
                part.at[h, other], from_z.at[h, k], s_z.at[h, k], r_z.at[h, k], chan=partner
            )

    y_copies = {}
    own = {}
    for h in (1, 0):
        for k in far_first + (0,):
            z_copies[h, k].wait_recv()
            both = part[h, along(k)] + from_z[h, k]
            if k == 0:
                own[h] = both
            else:
                z_sum[h, k] = both
                y_copies[h, k] = send(
                    z_sum.at[h, k], from_y.at[h, k], s_y.at[h, k], r_y.at[h, k], chan=along(k)
                )
    spread = jnp.dot(up[...], pool_picker(), preferred_element_type=f32) * 0.125
    gy, gz = {}, {}
    for h in (1, 0):
        for k in (1, 7, 2, 6, 3, 5, 4):
            y_copies[h, k].wait_recv()
            own[h] = own[h] + from_y[h, k]
        factor = jnp.where(own[h] > 0, 1.0, slope_neg)
        panel[h, chan] = (spread[:, h * 512 : h * 512 + 512] * factor).astype(bf16)
        block = panel.at[h, chan]
        for k in far_first:
            gy[h, k] = send(block, block, s_gy.at[h, k], r_gy.at[h, k], chan=along(k))
        gz[h, 0] = send(block, block, s_gz.at[h, 0], r_gz.at[h, 0], chan=partner)
    for h in (1, 0):
        for k in (1, 7, 2, 6, 3, 5, 4):
            gy[h, k].wait_recv()
            block = panel.at[h, before(k)]
            gz[h, k] = send(block, block, s_gz.at[h, k], r_gz.at[h, k], chan=partner)
    across = (((1,), (1,)), ((), ()))
    total = None
    grads = {}
    for h in (1, 0):
        for k in range(8):
            gz[h, k].wait_recv()
        if h == 0:
            first_plane = send(panel.at[0], rim_panel, s_rim.at[1], r_rim.at[1], space=ahead(n_space - 1))
        grads[h] = panel[h].reshape(128, 512)
        term = lax.dot_general(taps[h], grads[h], across, preferred_element_type=f32)
        total = term if total is None else total + term
    terms[0:27] = total.reshape(27, 8, 128)
    terms[27:32] = jnp.zeros((5, 8, 128), f32)
    rs = []
    for k in range(1, n_space):
        peer = ahead(k)
        rs.append(send(terms.at[peer], got.at[k], s_rs.at[k], r_rs.at[k], space=peer))

    for z in range(2):
        for q in range(4):
            folds[z * 4 + q] = jnp.dot(
                w, grads[z][:, q * 128 : q * 128 + 128], preferred_element_type=f32
            ).reshape(27, 8, 128)
    pre = side_by_side([own[0], own[1]])
    act = jnp.where(pre > 0, pre, slope_neg * pre)
    first = act.astype(bf16)
    rest = act - first.astype(f32)
    second = rest.astype(bf16)
    third = (rest - second.astype(f32)).astype(bf16)
    pick = pool_picker()
    mean = sum(
        lax.dot_general(piece, pick, across, preferred_element_type=f32)
        for piece in (third, second, first)
    )
    pooled[...] = (mean * 0.125).astype(bf16)
    first_plane.wait_recv()
    last = jnp.where(
        space < n_space - 1,
        jnp.dot(w, rim_panel[...].reshape(128, 512), preferred_element_type=f32),
        0.0,
    )
    for q in range(4):
        folds[8 + q] = last[:, q * 128 : q * 128 + 128].reshape(27, 8, 128)
    tall = []
    for b in range(3):
        for a in range(3):
            start = 4 if a == 0 else 0
            tall.append(
                side_by_side(
                    [
                        folds[start : start + 8, b * 9 + e * 3 + a].reshape(64, 128)
                        for e in range(3)
                    ]
                )
            )
    rows = jnp.concatenate(tall, axis=0)
    high = rows.astype(bf16)
    low = (rows - high.astype(f32)).astype(bf16)
    fold = lax.dot_general(high, pick_cols, across, preferred_element_type=f32)
    fold = fold + lax.dot_general(low, pick_cols, across, preferred_element_type=f32)
    fold = fold.reshape(3, 3, 2, 4, 8, 256)
    order = channel_first()
    depth_terms = (((1, 0),), ((2, 0), (0, 0)), ((1, 1),), ((2, 1), (0, 1)))
    for i in range(4):
        by_b = []
        for b in range(3):
            acc = None
            for a, zi in depth_terms[i]:
                acc = fold[b, a, zi] if acc is None else acc + fold[b, a, zi]
            by_b.append(acc)
        back, here, on = by_b
        shifted = jnp.concatenate([back[1:, :, :128], jnp.zeros((1, 8, 128), f32)], axis=0)
        plane = jnp.concatenate(
            [
                here[:, :, :128],
                on[:, :, :128] + back[:, :, 128:],
                here[:, :, 128:],
                on[:, :, 128:] + shifted,
            ],
            axis=0,
        ).reshape(128, 128)
        moved = jnp.dot(order, plane.astype(bf16), preferred_element_type=f32)
        grad_out[:, i] = moved.astype(bf16).reshape(8, 16, 128)

    share = terms[space]
    for k in range(1, n_space):
        rs[k - 1].wait_recv()
        share = share + got[k]
    mine[space] = share
    ag = []
    for k in range(1, n_space):
        block = mine.at[space]
        ag.append(send(block, block, s_ag.at[k], r_ag.at[k], space=ahead(k)))
    for copy in ag:
        copy.wait_recv()
    total_out[...] = mine[...]
    for copy in sent:
        copy.wait_send()


def in_vmem(count):
    return [pl.BlockSpec(memory_space=pltpu.VMEM)] * count


def shaped(*shape, dtype=f32):
    return jax.ShapeDtypeStruct(shape, dtype)


def block(vol, weights, up):
    n = lax.axis_size("space")
    dma = pltpu.SemaphoreType.DMA
    return pl.pallas_call(
        lambda *refs: block_kernel(n, *refs),
        name="block",
        out_shape=(
            shaped(8, 128, dtype=bf16),
            shaped(8, 4, 16, 128, dtype=bf16),
            shaped(n, 8, 128),
        ),
        in_specs=in_vmem(3),
        out_specs=tuple(in_vmem(3)),
        scratch_shapes=[
            pltpu.VMEM((8, 16, 128), bf16),
            pltpu.VMEM((27, 4, 8, 128), f32),
            pltpu.VMEM((2, 216, 512), bf16),
            pltpu.VMEM((2, 16, 8, 512), f32),
            pltpu.VMEM((2, 8, 8, 512), f32),
            pltpu.VMEM((2, 8, 8, 512), f32),
            pltpu.VMEM((2, 8, 8, 512), f32),
            pltpu.VMEM((2, 16, 8, 512), bf16),
            pltpu.VMEM((16, 8, 512), bf16),
            pltpu.VMEM((12, 27, 8, 128), f32),
            pltpu.VMEM((n, 8, 128), f32),
            pltpu.VMEM((n, 8, 128), f32),
            pltpu.VMEM((n, 8, 128), f32),
        ]
        + [dma((2,))] * 2
        + [dma((2, 8))] * 8
        + [dma((n,))] * 4,
        compiler_params=pltpu.CompilerParams(collective_id=0, has_side_effects=True),
    )(vol, weights, up)


def on_device(volume, kernel, upstream):
    weights = kernel.transpose(2, 3, 1, 0, 4).reshape(216, 128)
    pooled, input_grad, total = block(volume, weights, upstream.reshape(8, 128))
    kernel_grad = total[:27].reshape(3, 3, 3, 8, 128).transpose(3, 2, 0, 1, 4)
    return pooled.reshape(upstream.shape), input_grad, kernel_grad


def solution(mesh):
    return jax.shard_map(
        on_device,
        mesh=mesh,
        in_specs=(
            P("chan", "space", None, None),
            P("chan", None, None, None, None),
            P("chan", "space", None, None),
        ),
        out_specs=(
            P("chan", "space", None, None),
            P("chan", "space", None, None),
            P("chan", None, None, None, None),
        ),
        check_vma=False,
    )
```

time: 440 us -> 60.6 us (0.14)
  waiting for transfers between devices: 296 us -> 0 us
  blocking collectives: 63.1 us -> 0 us
  Pallas kernels: 0 us -> 54 us
  matrix products: 24.3 us -> 0 us
  local copies, waits for them, and re-layouts: 24.7 us -> 5.69 us
  starting transfers between devices: 16.3 us -> 0 us
  between operations: 14.3 us -> 0.65 us
    psum x1 -> x0, waiting for transfers between devices: 262 us -> none  [on_device(): kernel_grad = lax.psum(weight_grad, 'space')]
    all_gather x2 -> x0, blocking collectives: 63.1 us -> none  [the longest x1 33 us: on_device(): lax.all_gather(kernel, 'chan', axis=0, tiled=True)]
    pallas_call x0 -> x1, Pallas kernels: none -> 54 us  [block(): pl.pallas_call(lambda *refs: block_kernel(n, *refs), name='block', out_sh...]
    all_gather x1 -> x0, waiting for transfers between devices: 27.8 us -> none  [on_device(): lax.all_gather(padded, 'chan', axis=0, tiled=True)]
    ppermute x2 -> x0, starting transfers between devices: 16.2 us -> none  [from_behind(): return lax.ppermute(block, axis, route)]
    conv_general_dilated x2 -> x0, matrix products: 16 us -> none  [the longest x1 13.7 us: on_device(): lax.conv_general_dilated(padded[None], panel[:, :out_depth][None], (1, 1,...]
    broadcast_in_dim x6 -> x0, local copies, waits for them, and re-layouts: 8.62 us -> none  [the longest x1 7.83 us: on_device(): padded[None]]
    dot_general x27 -> x0, matrix products: 8.32 us -> none  [on_device(): jnp.einsum('co,ozyx->czyx', columns[:, depth_tap, row_tap, col_tap, :], s...]
  transfers between devices with their start and end apart: 4 -> 0, of which waited for: 4 -> 0; matrix products, arithmetic and copies ran while one was open for 4% -> 0% of each run, Pallas kernels for 0% -> 0%
where the time goes in v2:
time: 60.6 us; the launch traced here: 60.3 us
  Pallas kernels  54 us (89%)
  local copies, waits for them, and re-layouts  5.69 us (9%)
  between operations  0.65 us (1%)
    pallas_call x1, Pallas kernels, block(): pl.pallas_call(lambda *refs: block_kernel(n, *refs), name='block', out_sh...  54 us
    transpose x1, local copies, waits for them, and re-layouts, on_device(): weights = kernel.transpose(2, 3, 1, 0, 4).reshape(216, 128)  1.45 us
    unnamed x7, local copies, waits for them, and re-layouts  1.34 us

profile of v2, /device:TPU:1, one launch (start us, length us, event | category | flops | bytes accessed | tf_op | source)
XLA Modules:
  0.0 60.3 jit_solution(6840194870303687329)
XLA Ops:
  0.6 0.0 copy-start.1
  0.6 1.5 %copy.6 = bf16[3,3,3,8,128]{4,3,2,1,0:T(8,128)(2,1)} copy(bf16[3,3,3,8,128]{4,3,1,0,2:T(8,128)(2,1)} %bitcast.10) | data formatting | bytes 110592 | tf_op jit(solution)/shard_map/transpose | solution.py:336
  2.1 0.0 copy-done.1
  2.1 0.7 %reshape.19.refs_2_ = bf16[8,128]{1,0:T(8,128)(2,1)} reshape(bf16[8,1,4,32]{3,2,1,0:T(4,128)(2,1)S(1)} %copy-done.1) | data formatting | bytes 4096 | tf_op jit(solution)/shard_map/reshape | solution.py:337
  2.8 54.0 %block.1 = (bf16[8,128]{1,0:T(8,128)(2,1)}, bf16[8,4,16,128]{3,2,1,0:T(8,128)(2,1)}, f32[32,8,128]{2,1,0:T(8,128)}) custom-call(bf16[8,4,16,128]{3,2,1,0:T(8,128)(2,1)} %refs_0_.1, bf16[216,128]{1,0:T(8,128)(2,1)} %bitcast.8, bf16[8,128]{1,0:T(8,128)(2,1)} %reshape.19.refs_2_), custom_call_target="tpu_custom_call" | custom-call | tf_op jit(solution)/shard_map/block/pallas_call | solution.py:303
  56.7 0.9 %slice.3 = f32[27,8,128]{2,1,0:T(8,128)S(1)} slice(f32[32,8,128]{2,1,0:T(8,128)} %get-tuple-element.8), slice={[0:27], [0:8], [0:128]} | slice | bytes 221184 | tf_op jit(solution)/shard_map/slice | solution.py:338
  57.7 0.0 copy-start
  57.7 0.7 %copy.10 = f32[3,3,3,8,128]{4,3,1,0,2:T(8,128)} copy(f32[3,3,3,8,128]{4,3,2,1,0:T(8,128)S(1)} %bitcast.7) | data formatting | bytes 221184 | tf_op jit(solution)/shard_map/reshape | solution.py:338
  58.3 0.0 copy-start.2
  58.3 0.7 %copy-done.2 = bf16[8,128]{1,0:T(8,128)(2,1)S(1)} copy-done((bf16[8,128]{1,0:T(8,128)(2,1)S(1)}, bf16[8,128]{1,0:T(8,128)(2,1)}, u32[]{:S(2)}) %copy-start.2) | copy-done | bytes 2072
  59.0 0.7 %reshape.20 = bf16[8,1,4,32]{3,2,0,1:T(4,128)(2,1)} reshape(bf16[8,128]{1,0:T(8,128)(2,1)S(1)} %copy-done.2) | data formatting | bytes 4096 | tf_op jit(solution)/shard_map/reshape | solution.py:339
  59.7 0.0 copy-done
  59.7 0.7 %copy.12 = bf16[8,4,16,128]{3,2,1,0:T(8,128)(2,1)} copy(bf16[8,4,16,128]{3,2,1,0:T(8,128)(2,1)S(1)} %copy-done) | data formatting | bytes 262144
Async XLA Ops:
  0.6 1.5 %copy-start.1 = (bf16[8,1,4,32]{3,2,1,0:T(4,128)(2,1)S(1)}, bf16[8,1,4,32]{3,2,1,0:T(4,128)(2,1)}, u32[]{:S(2)}) copy-start(bf16[8,1,4,32]{3,2,1,0:T(4,128)(2,1)} %param.5) | copy-start | bytes 6148
  57.7 2.0 %copy-start = (bf16[8,4,16,128]{3,2,1,0:T(8,128)(2,1)S(1)}, bf16[8,4,16,128]{3,2,1,0:T(8,128)(2,1)}, u32[]{:S(2)}) copy-start(bf16[8,4,16,128]{3,2,1,0:T(8,128)(2,1)} %get-tuple-element.16) | copy-start | bytes 393220
  58.3 0.7 %copy-start.2 = (bf16[8,128]{1,0:T(8,128)(2,1)S(1)}, bf16[8,128]{1,0:T(8,128)(2,1)}, u32[]{:S(2)}) copy-start(bf16[8,128]{1,0:T(8,128)(2,1)} %get-tuple-element.6) | copy-start | bytes 6148

commit v3 on v2

--- a/solution.py
+++ b/solution.py
@@ -146,9 +146,8 @@
             )
             picked = jnp.dot(pairs, pick_cols, preferred_element_type=f32)
             for e in range(3):
-                tap = b * 9 + e * 3
-                stage[tap : tap + 3] = picked[:, e * 128 : e * 128 + 128].reshape(3, 4, 8, 128)
-        columns = side_by_side([stage[:, q].reshape(216, 128) for q in range(4)]).astype(bf16)
+                stage[:, b * 3 + e] = picked[:, e * 128 : e * 128 + 128].reshape(3, 4, 8, 128)
+        columns = side_by_side([stage[:, :, q].reshape(216, 128) for q in range(4)]).astype(bf16)
         taps[h] = columns
         part[h] = lax.dot_general(
             w, columns, (((0,), (0,)), ((), ())), preferred_element_type=f32
@@ -172,7 +171,9 @@
                 y_copies[h, k] = send(
                     z_sum.at[h, k], from_y.at[h, k], s_y.at[h, k], r_y.at[h, k], chan=along(k)
                 )
-    spread = jnp.dot(up[...], pool_picker(), preferred_element_type=f32) * 0.125
+    coarse = up[...].astype(f32).reshape(8, 4, 32)
+    flat = side_by_side([coarse[:, q] for q in range(4)]).astype(bf16)
+    spread = jnp.dot(flat, pool_picker(), preferred_element_type=f32) * 0.125
     gy, gz = {}, {}
     for h in (1, 0):
         for k in (1, 7, 2, 6, 3, 5, 4):
@@ -223,7 +224,8 @@
         lax.dot_general(piece, pick, across, preferred_element_type=f32)
         for piece in (third, second, first)
     )
-    pooled[...] = (mean * 0.125).astype(bf16)
+    mean = jnp.stack([mean[:, q * 32 : q * 32 + 32] for q in range(4)], axis=1)
+    pooled[...] = (mean * 0.125).astype(bf16).reshape(8, 1, 4, 32)
     first_plane.wait_recv()
     last = jnp.where(
         space < n_space - 1,
@@ -239,7 +241,7 @@
             tall.append(
                 side_by_side(
                     [
-                        folds[start : start + 8, b * 9 + e * 3 + a].reshape(64, 128)
+                        folds[start : start + 8, a * 9 + b * 3 + e].reshape(64, 128)
                         for e in range(3)
                     ]
                 )
@@ -284,7 +286,7 @@
         ag.append(send(block, block, s_ag.at[k], r_ag.at[k], space=ahead(k)))
     for copy in ag:
         copy.wait_recv()
-    total_out[...] = mine[...]
+    total_out[...] = mine[0:27]
     for copy in sent:
         copy.wait_send()
 
@@ -304,15 +306,15 @@
         lambda *refs: block_kernel(n, *refs),
         name="block",
         out_shape=(
-            shaped(8, 128, dtype=bf16),
+            shaped(8, 1, 4, 32, dtype=bf16),
             shaped(8, 4, 16, 128, dtype=bf16),
-            shaped(n, 8, 128),
+            shaped(27, 8, 128),
         ),
         in_specs=in_vmem(3),
         out_specs=tuple(in_vmem(3)),
         scratch_shapes=[
             pltpu.VMEM((8, 16, 128), bf16),
-            pltpu.VMEM((27, 4, 8, 128), f32),
+            pltpu.VMEM((3, 9, 4, 8, 128), f32),
             pltpu.VMEM((2, 216, 512), bf16),
             pltpu.VMEM((2, 16, 8, 512), f32),
             pltpu.VMEM((2, 8, 8, 512), f32),
@@ -333,10 +335,10 @@
 
 
 def on_device(volume, kernel, upstream):
-    weights = kernel.transpose(2, 3, 1, 0, 4).reshape(216, 128)
-    pooled, input_grad, total = block(volume, weights, upstream.reshape(8, 128))
-    kernel_grad = total[:27].reshape(3, 3, 3, 8, 128).transpose(3, 2, 0, 1, 4)
-    return pooled.reshape(upstream.shape), input_grad, kernel_grad
+    weights = kernel.transpose(1, 2, 3, 0, 4).reshape(216, 128)
+    pooled, input_grad, total = block(volume, weights, upstream)
+    kernel_grad = total.reshape(3, 3, 3, 8, 128).transpose(3, 0, 1, 2, 4)
+    return pooled, input_grad, kernel_grad
 
 
 def solution(mesh):

time: 60.6 us -> 58.2 us (0.960)
  local copies, waits for them, and re-layouts: 5.69 us -> 3.55 us
    unnamed x7 -> x5, local copies, waits for them, and re-layouts: 1.34 us -> 3.55 us
    reshape x3 -> x0, local copies, waits for them, and re-layouts: 1.99 us -> none  [the longest x1 0.68 us: on_device(): return (pooled.reshape(upstream.shape), input_grad, kernel_grad)]
    transpose x1 -> x0, local copies, waits for them, and re-layouts: 1.45 us -> none  [on_device(): weights = kernel.transpose(2, 3, 1, 0, 4).reshape(216, 128)]
    slice x1 -> x0, local copies, waits for them, and re-layouts: 0.91 us -> none  [on_device(): kernel_grad = total[:27].reshape(3, 3, 3, 8, 128).transpose(3, 2, 0, 1, 4)]
where the time goes in v3:
time: 58.2 us; the launch traced here: 58 us
  Pallas kernels  53.8 us (92%)
  local copies, waits for them, and re-layouts  3.55 us (6%)
  between operations  0.64 us (1%)
    pallas_call x1, Pallas kernels, block(): pl.pallas_call(lambda *refs: block_kernel(n, *refs), name='block', out_sh...  53.8 us
    unnamed x5, local copies, waits for them, and re-layouts  3.55 us

profile of v3, /device:TPU:1, one launch (start us, length us, event | category | flops | bytes accessed | tf_op | source)
XLA Modules:
  0.0 58.0 jit_solution(4989708573880894101)
XLA Ops:
  0.6 53.8 %block.1 = (bf16[8,1,4,32]{3,2,1,0:T(4,128)(2,1)}, bf16[8,4,16,128]{3,2,1,0:T(8,128)(2,1)}, f32[27,8,128]{2,1,0:T(8,128)}) custom-call(bf16[8,4,16,128]{3,2,1,0:T(8,128)(2,1)} %refs_0_.1, bf16[216,128]{1,0:T(8,128)(2,1)} %bitcast.7, bf16[8,1,4,32]{3,2,1,0:T(4,128)(2,1)} %refs_2_.1), custom_call_target="tpu_custom_call" | custom-call | tf_op jit(solution)/shard_map/block/pallas_call | solution.py:305
  54.4 1.3 %copy.9 = bf16[8,1,4,32]{3,2,1,0:T(4,128)(2,1)} copy(bf16[8,1,4,32]{3,2,1,0:T(4,128)(2,1)} %get-tuple-element.12) | data formatting | bytes 4096
  55.7 0.0 copy-start
  55.7 1.6 %copy.10 = bf16[8,4,16,128]{3,2,1,0:T(8,128)(2,1)} copy(bf16[8,4,16,128]{3,2,1,0:T(8,128)(2,1)} %get-tuple-element.13) | data formatting | bytes 262144
  57.3 0.0 copy-done
  57.3 0.6 %copy.11 = f32[8,3,3,3,128]{4,0,3,2,1:T(8,128)} copy(f32[8,3,3,3,128]{4,0,3,2,1:T(8,128)S(1)} %bitcast.6) | data formatting | bytes 221184
Async XLA Ops:
  55.7 1.6 %copy-start = (f32[27,8,128]{2,1,0:T(8,128)S(1)}, f32[27,8,128]{2,1,0:T(8,128)}, u32[]{:S(2)}) copy-start(f32[27,8,128]{2,1,0:T(8,128)} %get-tuple-element.8) | copy-start | bytes 331780

commit v4 on v3

--- a/solution.py
+++ b/solution.py
@@ -56,6 +56,7 @@
     grad_out,
     total_out,
     rim,
+    spread,
     stage,
     taps,
     part,
@@ -80,6 +81,8 @@
     r_gz,
     s_rs,
     r_rs,
+    s_up,
+    r_up,
     s_ag,
     r_ag,
 ):
@@ -90,6 +93,9 @@
 
     def along(k):
         return half * 8 + lax.rem(place + k, 8)
+
+    def opposite(k):
+        return (1 - half) * 8 + lax.rem(place + k, 8)
 
     def before(k):
         return half * 8 + lax.rem(place + 8 - k, 8)
@@ -115,7 +121,8 @@
     barrier = pltpu.get_barrier_semaphore()
     for k in range(1, 8):
         pl.semaphore_signal(barrier, inc=1, device_id={"chan": along(k)}, device_id_type=MESH)
-    pl.semaphore_signal(barrier, inc=1, device_id={"chan": partner}, device_id_type=MESH)
+    for k in (0, 3, 4, 5):
+        pl.semaphore_signal(barrier, inc=1, device_id={"chan": opposite(k)}, device_id_type=MESH)
     for k in range(1, n_space):
         pl.semaphore_signal(barrier, inc=1, device_id={"space": ahead(k)}, device_id_type=MESH)
 
@@ -126,37 +133,53 @@
         return jnp.dot(pick_rows, plane.reshape(128, 128), preferred_element_type=f32)
 
     planes = [None] + [rows_of(vol[:, p]).astype(bf16) for p in range(4)]
-    pl.semaphore_wait(barrier, 8 + n_space - 1)
-    rim_copy = send(vol.at[:, 3], rim, s_rim.at[0], r_rim.at[0], space=ahead(1))
-
-    far_first = (4, 3, 5, 2, 6, 1, 7)
     w = weights[...]
-    z_copies = {}
-    for h in (1, 0):
-        if h == 0:
-            rim_copy.wait_recv()
-            planes[0] = jnp.where(space > 0, rows_of(rim[...]), 0.0).astype(bf16)
+
+    def fill(used, first):
+        count = len(used)
         for b in range(3):
             pairs = jnp.concatenate(
                 [
                     side_by_side([u[32 * b : 32 * b + 32], u[32 * b + 64 : 32 * b + 96]])
-                    for u in planes[2 * h : 2 * h + 3]
+                    for u in used
                 ],
                 axis=0,
             )
             picked = jnp.dot(pairs, pick_cols, preferred_element_type=f32)
             for e in range(3):
-                stage[:, b * 3 + e] = picked[:, e * 128 : e * 128 + 128].reshape(3, 4, 8, 128)
+                stage[first : first + count, b * 3 + e] = picked[
+                    :, e * 128 : e * 128 + 128
+                ].reshape(count, 4, 8, 128)
+
+    def multiply(h):
         columns = side_by_side([stage[:, :, q].reshape(216, 128) for q in range(4)]).astype(bf16)
         taps[h] = columns
         part[h] = lax.dot_general(
             w, columns, (((0,), (0,)), ((), ())), preferred_element_type=f32
         ).reshape(16, 8, 512)
+
+    far_first = (4, 3, 5, 2, 6, 1, 7)
+    z_copies = {}
+
+    def send_half(h):
         for k in far_first + (0,):
-            other = (1 - half) * 8 + lax.rem(place + k, 8)
             z_copies[h, k] = send(
-                part.at[h, other], from_z.at[h, k], s_z.at[h, k], r_z.at[h, k], chan=partner
+                part.at[h, opposite(k)], from_z.at[h, k], s_z.at[h, k], r_z.at[h, k], chan=partner
             )
+
+    fill(planes[2:5], 0)
+    multiply(1)
+    fill(planes[1:3], 1)
+    coarse = up[...].astype(f32).reshape(8, 4, 32)
+    flat = side_by_side([coarse[:, q] for q in range(4)]).astype(bf16)
+    spread[...] = jnp.dot(flat, pool_picker(), preferred_element_type=f32) * 0.125
+    pl.semaphore_wait(barrier, 7 + 4 + n_space - 1)
+    rim_copy = send(vol.at[:, 3], rim, s_rim.at[0], r_rim.at[0], space=ahead(1))
+    send_half(1)
+    rim_copy.wait_recv()
+    fill([jnp.where(space > 0, rows_of(rim[...]), 0.0).astype(bf16)], 0)
+    multiply(0)
+    send_half(0)
 
     y_copies = {}
     own = {}
@@ -171,9 +194,6 @@
                 y_copies[h, k] = send(
                     z_sum.at[h, k], from_y.at[h, k], s_y.at[h, k], r_y.at[h, k], chan=along(k)
                 )
-    coarse = up[...].astype(f32).reshape(8, 4, 32)
-    flat = side_by_side([coarse[:, q] for q in range(4)]).astype(bf16)
-    spread = jnp.dot(flat, pool_picker(), preferred_element_type=f32) * 0.125
     gy, gz = {}, {}
     for h in (1, 0):
         for k in (1, 7, 2, 6, 3, 5, 4):
@@ -184,9 +204,10 @@
         block = panel.at[h, chan]
         for k in far_first:
             gy[h, k] = send(block, block, s_gy.at[h, k], r_gy.at[h, k], chan=along(k))
-        gz[h, 0] = send(block, block, s_gz.at[h, 0], r_gz.at[h, 0], chan=partner)
+        for k in (4, 3, 5, 0):
+            gz[h, k] = send(block, block, s_gz.at[h, k], r_gz.at[h, k], chan=opposite(k))
     for h in (1, 0):
-        for k in (1, 7, 2, 6, 3, 5, 4):
+        for k in (1, 7, 2, 6):
             gy[h, k].wait_recv()
             block = panel.at[h, before(k)]
             gz[h, k] = send(block, block, s_gz.at[h, k], r_gz.at[h, k], chan=partner)
@@ -194,6 +215,8 @@
     total = None
     grads = {}
     for h in (1, 0):
+        for k in (3, 5, 4):
+            gy[h, k].wait_recv()
         for k in range(8):
             gz[h, k].wait_recv()
         if h == 0:
@@ -280,11 +303,22 @@
         rs[k - 1].wait_recv()
         share = share + got[k]
     mine[space] = share
-    ag = []
-    for k in range(1, n_space):
+    layers = n_space // 8
+    layer = lax.div(space, 8)
+    slot = lax.rem(space, 8)
+    hops = {}
+    for k in range(1, layers):
         block = mine.at[space]
-        ag.append(send(block, block, s_ag.at[k], r_ag.at[k], space=ahead(k)))
-    for copy in ag:
+        hops[k] = send(block, block, s_up.at[k], r_up.at[k], space=lax.rem(space + 8 * k, n_space))
+    spreads = []
+    for k in range(layers):
+        if k > 0:
+            hops[k].wait_recv()
+        block = mine.at[lax.rem(space + n_space - 8 * k, n_space)]
+        for m in range(1, 8):
+            peer = layer * 8 + lax.rem(slot + m, 8)
+            spreads.append(send(block, block, s_ag.at[k, m], r_ag.at[k, m], space=peer))
+    for copy in spreads:
         copy.wait_recv()
     total_out[...] = mine[0:27]
     for copy in sent:
@@ -314,6 +348,7 @@
         out_specs=tuple(in_vmem(3)),
         scratch_shapes=[
             pltpu.VMEM((8, 16, 128), bf16),
+            pltpu.VMEM((8, 1024), f32),
             pltpu.VMEM((3, 9, 4, 8, 128), f32),
             pltpu.VMEM((2, 216, 512), bf16),
             pltpu.VMEM((2, 16, 8, 512), f32),
@@ -329,14 +364,30 @@
         ]
         + [dma((2,))] * 2
         + [dma((2, 8))] * 8
-        + [dma((n,))] * 4,
+        + [dma((n,))] * 2
+        + [dma((n // 8,))] * 2
+        + [dma((n // 8, 8))] * 2,
         compiler_params=pltpu.CompilerParams(collective_id=0, has_side_effects=True),
     )(vol, weights, up)
 
 
+def hand_over(*arrays):
+    def kernel(*refs):
+        for source, target in zip(refs[:3], refs[3:]):
+            target[...] = source[...]
+
+    return pl.pallas_call(
+        kernel,
+        name="hand_over",
+        out_shape=tuple(jax.ShapeDtypeStruct(x.shape, x.dtype) for x in arrays),
+        in_specs=in_vmem(3),
+        out_specs=tuple(in_vmem(3)),
+    )(*arrays)
+
+
 def on_device(volume, kernel, upstream):
     weights = kernel.transpose(1, 2, 3, 0, 4).reshape(216, 128)
-    pooled, input_grad, total = block(volume, weights, upstream)
+    pooled, input_grad, total = hand_over(*block(volume, weights, upstream))
     kernel_grad = total.reshape(3, 3, 3, 8, 128).transpose(3, 0, 1, 2, 4)
     return pooled, input_grad, kernel_grad
 

time: 58.2 us -> 58.1 us (level)
  local copies, waits for them, and re-layouts: 3.55 us -> 0 us
  Pallas kernels: 53.8 us -> 57.3 us
    unnamed x5 -> x0, local copies, waits for them, and re-layouts: 3.55 us -> none
    pallas_call x1, Pallas kernels: 53.8 us -> 55.7 us  [block(): pl.pallas_call(lambda *refs: block_kernel(n, *refs), name='block', out_sh...]
    pallas_call x0 -> x1, Pallas kernels: none -> 1.68 us  [hand_over(): pl.pallas_call(kernel, name='hand_over', out_shape=tuple((jax.ShapeDtypeS...]
where the time goes in v4:
time: 58.1 us; the launch traced here: 58 us
  Pallas kernels  57.3 us (99%)
  between operations  0.64 us (1%)
    pallas_call x1, Pallas kernels, block(): pl.pallas_call(lambda *refs: block_kernel(n, *refs), name='block', out_sh...  55.7 us
    pallas_call x1, Pallas kernels, hand_over(): pl.pallas_call(kernel, name='hand_over', out_shape=tuple((jax.ShapeDtypeS...  1.68 us

profile of v4, /device:TPU:1, one launch (start us, length us, event | category | flops | bytes accessed | tf_op | source)
XLA Modules:
  0.0 58.0 jit_solution(6810121892707005275)
XLA Ops:
  0.6 55.7 %block.1 = (bf16[8,1,4,32]{3,2,1,0:T(4,128)(2,1)}, bf16[8,4,16,128]{3,2,1,0:T(8,128)(2,1)}, f32[27,8,128]{2,1,0:T(8,128)}) custom-call(bf16[8,4,16,128]{3,2,1,0:T(8,128)(2,1)} %refs_0_.1, bf16[216,128]{1,0:T(8,128)(2,1)} %bitcast.6, bf16[8,1,4,32]{3,2,1,0:T(4,128)(2,1)} %refs_2_.1), custom_call_target="tpu_custom_call" | custom-call | tf_op jit(solution)/shard_map/block/pallas_call | solution.py:339
  56.3 1.7 %hand_over.1 = (bf16[8,1,4,32]{3,2,1,0:T(4,128)(2,1)}, bf16[8,4,16,128]{3,2,1,0:T(8,128)(2,1)}, f32[27,8,128]{2,1,0:T(8,128)}) custom-call(bf16[8,1,4,32]{3,2,1,0:T(4,128)(2,1)} %get-tuple-element.9.refs_0_, bf16[8,4,16,128]{3,2,1,0:T(8,128)(2,1)} %get-tuple-element.10.refs_1_, f32[27,8,128]{2,1,0:T(8,128)} %get-tuple-element.11.refs_2_), custom_call_target="tpu_custom_call" | custom-call | tf_op jit(solution)/shard_map/hand_over/pallas_call | solution.py:379

commit v5 on v4

--- a/solution.py
+++ b/solution.py
@@ -68,6 +68,7 @@
     folds,
     terms,
     got,
+    layer_sums,
     mine,
     s_rim,
     r_rim,
@@ -123,7 +124,17 @@
         pl.semaphore_signal(barrier, inc=1, device_id={"chan": along(k)}, device_id_type=MESH)
     for k in (0, 3, 4, 5):
         pl.semaphore_signal(barrier, inc=1, device_id={"chan": opposite(k)}, device_id_type=MESH)
-    for k in range(1, n_space):
+    layers = n_space // 8
+    layer = lax.div(space, 8)
+    slot = lax.rem(space, 8)
+
+    def beside(m):
+        return lax.rem(slot + m, 8)
+
+    for m in range(1, 8):
+        peer = layer * 8 + beside(m)
+        pl.semaphore_signal(barrier, inc=1, device_id={"space": peer}, device_id_type=MESH)
+    for k in [8 * k for k in range(1, layers)] + [1, n_space - 1]:
         pl.semaphore_signal(barrier, inc=1, device_id={"space": ahead(k)}, device_id_type=MESH)
 
     pick_rows = row_picker()
@@ -151,11 +162,14 @@
                     :, e * 128 : e * 128 + 128
                 ].reshape(count, 4, 8, 128)
 
-    def multiply(h):
-        columns = side_by_side([stage[:, :, q].reshape(216, 128) for q in range(4)]).astype(bf16)
-        taps[h] = columns
-        part[h] = lax.dot_general(
-            w, columns, (((0,), (0,)), ((), ())), preferred_element_type=f32
+    def columns_of(count):
+        return side_by_side(
+            [stage[0:count, :, q].reshape(72 * count, 128) for q in range(4)]
+        ).astype(bf16)
+
+    def multiply(rows, columns):
+        return lax.dot_general(
+            rows, columns, (((0,), (0,)), ((), ())), preferred_element_type=f32
         ).reshape(16, 8, 512)
 
     far_first = (4, 3, 5, 2, 6, 1, 7)
@@ -168,18 +182,24 @@
             )
 
     fill(planes[2:5], 0)
-    multiply(1)
+    columns = columns_of(3)
+    taps[1] = columns
+    part[1] = multiply(w, columns)
+    stage[0:1] = jnp.zeros((1, 9, 4, 8, 128), f32)
     fill(planes[1:3], 1)
+    part[0] = multiply(w, columns_of(3))
+    w_rim = w[0:72]
     coarse = up[...].astype(f32).reshape(8, 4, 32)
     flat = side_by_side([coarse[:, q] for q in range(4)]).astype(bf16)
     spread[...] = jnp.dot(flat, pool_picker(), preferred_element_type=f32) * 0.125
-    pl.semaphore_wait(barrier, 7 + 4 + n_space - 1)
+    pl.semaphore_wait(barrier, 7 + 4 + 7 + layers - 1 + 2)
     rim_copy = send(vol.at[:, 3], rim, s_rim.at[0], r_rim.at[0], space=ahead(1))
     send_half(1)
     rim_copy.wait_recv()
     fill([jnp.where(space > 0, rows_of(rim[...]), 0.0).astype(bf16)], 0)
-    multiply(0)
+    part[0] = part[0] + multiply(w_rim, columns_of(1))
     send_half(0)
+    taps[0] = columns_of(3)
 
     y_copies = {}
     own = {}
@@ -224,12 +244,11 @@
         grads[h] = panel[h].reshape(128, 512)
         term = lax.dot_general(taps[h], grads[h], across, preferred_element_type=f32)
         total = term if total is None else total + term
-    terms[0:27] = total.reshape(27, 8, 128)
-    terms[27:32] = jnp.zeros((5, 8, 128), f32)
+    terms[...] = jnp.concatenate([total, jnp.zeros((40, 128), f32)], axis=0).reshape(8, 32, 128)
     rs = []
-    for k in range(1, n_space):
-        peer = ahead(k)
-        rs.append(send(terms.at[peer], got.at[k], s_rs.at[k], r_rs.at[k], space=peer))
+    for m in (3, 4, 5, 2, 6, 1, 7):
+        peer = layer * 8 + beside(m)
+        rs.append(send(terms.at[beside(m)], got.at[m], s_rs.at[m], r_rs.at[m], space=peer))
 
     for z in range(2):
         for q in range(4):
@@ -249,6 +268,16 @@
     )
     mean = jnp.stack([mean[:, q * 32 : q * 32 + 32] for q in range(4)], axis=1)
     pooled[...] = (mean * 0.125).astype(bf16).reshape(8, 1, 4, 32)
+    share = terms[slot]
+    for copy in rs:
+        copy.wait_recv()
+    for m in range(1, 8):
+        share = share + got[m]
+    layer_sums[layer] = share
+    ups = []
+    for k in range(1, layers):
+        block = layer_sums.at[layer]
+        ups.append(send(block, block, s_up.at[k], r_up.at[k], space=ahead(8 * k)))
     first_plane.wait_recv()
     last = jnp.where(
         space < n_space - 1,
@@ -274,6 +303,16 @@
     low = (rows - high.astype(f32)).astype(bf16)
     fold = lax.dot_general(high, pick_cols, across, preferred_element_type=f32)
     fold = fold + lax.dot_general(low, pick_cols, across, preferred_element_type=f32)
+    for copy in ups:
+        copy.wait_recv()
+    share = layer_sums[0]
+    for k in range(1, layers):
+        share = share + layer_sums[k]
+    mine[slot] = share
+    ag = []
+    for m in (3, 4, 5, 2, 6, 1, 7):
+        block = mine.at[slot]
+        ag.append(send(block, block, s_ag.at[m], r_ag.at[m], space=layer * 8 + beside(m)))
     fold = fold.reshape(3, 3, 2, 4, 8, 256)
     order = channel_first()
     depth_terms = (((1, 0),), ((2, 0), (0, 0)), ((1, 1),), ((2, 1), (0, 1)))
@@ -298,29 +337,10 @@
         moved = jnp.dot(order, plane.astype(bf16), preferred_element_type=f32)
         grad_out[:, i] = moved.astype(bf16).reshape(8, 16, 128)
 
-    share = terms[space]
-    for k in range(1, n_space):
-        rs[k - 1].wait_recv()
-        share = share + got[k]
-    mine[space] = share
-    layers = n_space // 8
-    layer = lax.div(space, 8)
-    slot = lax.rem(space, 8)
-    hops = {}
-    for k in range(1, layers):
-        block = mine.at[space]
-        hops[k] = send(block, block, s_up.at[k], r_up.at[k], space=lax.rem(space + 8 * k, n_space))
-    spreads = []
-    for k in range(layers):
-        if k > 0:
-            hops[k].wait_recv()
-        block = mine.at[lax.rem(space + n_space - 8 * k, n_space)]
-        for m in range(1, 8):
-            peer = layer * 8 + lax.rem(slot + m, 8)
-            spreads.append(send(block, block, s_ag.at[k, m], r_ag.at[k, m], space=peer))
-    for copy in spreads:
+    for copy in ag:
         copy.wait_recv()
-    total_out[...] = mine[0:27]
+    for m in range(7):
+        total_out[4 * m : min(4 * m + 4, 27)] = mine[m].reshape(4, 8, 128)[: min(4, 27 - 4 * m)]
     for copy in sent:
         copy.wait_send()
 
@@ -358,15 +378,16 @@
             pltpu.VMEM((2, 16, 8, 512), bf16),
             pltpu.VMEM((16, 8, 512), bf16),
             pltpu.VMEM((12, 27, 8, 128), f32),
-            pltpu.VMEM((n, 8, 128), f32),
-            pltpu.VMEM((n, 8, 128), f32),
-            pltpu.VMEM((n, 8, 128), f32),
+            pltpu.VMEM((8, 32, 128), f32),
+            pltpu.VMEM((8, 32, 128), f32),
+            pltpu.VMEM((n // 8, 32, 128), f32),
+            pltpu.VMEM((8, 32, 128), f32),
         ]
         + [dma((2,))] * 2
         + [dma((2, 8))] * 8
-        + [dma((n,))] * 2
+        + [dma((8,))] * 2
         + [dma((n // 8,))] * 2
-        + [dma((n // 8, 8))] * 2,
+        + [dma((8,))] * 2,
         compiler_params=pltpu.CompilerParams(collective_id=0, has_side_effects=True),
     )(vol, weights, up)
 

time: 58.1 us -> 54.1 us (0.931)
  Pallas kernels: 57.3 us -> 53.3 us
    pallas_call x1, Pallas kernels: 55.7 us -> 51.6 us  [block(): pl.pallas_call(lambda *refs: block_kernel(n, *refs), name='block', out_sh...]
where the time goes in v5:
time: 54.1 us; the launch traced here: 54 us
  Pallas kernels  53.3 us (99%)
  between operations  0.64 us (1%)
    pallas_call x1, Pallas kernels, block(): pl.pallas_call(lambda *refs: block_kernel(n, *refs), name='block', out_sh...  51.6 us
    pallas_call x1, Pallas kernels, hand_over(): pl.pallas_call(kernel, name='hand_over', out_shape=tuple((jax.ShapeDtypeS...  1.68 us

profile of v5, /device:TPU:1, one launch (start us, length us, event | category | flops | bytes accessed | tf_op | source)
XLA Modules:
  0.0 54.0 jit_solution(14641308729557698368)
XLA Ops:
  0.6 51.6 %block.1 = (bf16[8,1,4,32]{3,2,1,0:T(4,128)(2,1)}, bf16[8,4,16,128]{3,2,1,0:T(8,128)(2,1)}, f32[27,8,128]{2,1,0:T(8,128)}) custom-call(bf16[8,4,16,128]{3,2,1,0:T(8,128)(2,1)} %refs_0_.1, bf16[216,128]{1,0:T(8,128)(2,1)} %bitcast.6, bf16[8,1,4,32]{3,2,1,0:T(4,128)(2,1)} %refs_2_.1), custom_call_target="tpu_custom_call" | custom-call | tf_op jit(solution)/shard_map/block/pallas_call | solution.py:359
  52.3 1.7 %hand_over.1 = (bf16[8,1,4,32]{3,2,1,0:T(4,128)(2,1)}, bf16[8,4,16,128]{3,2,1,0:T(8,128)(2,1)}, f32[27,8,128]{2,1,0:T(8,128)}) custom-call(bf16[8,1,4,32]{3,2,1,0:T(4,128)(2,1)} %get-tuple-element.9.refs_0_, bf16[8,4,16,128]{3,2,1,0:T(8,128)(2,1)} %get-tuple-element.10.refs_1_, f32[27,8,128]{2,1,0:T(8,128)} %get-tuple-element.11.refs_2_), custom_call_target="tpu_custom_call" | custom-call | tf_op jit(solution)/shard_map/hand_over/pallas_call | solution.py:400

commit v6 on v5

--- a/solution.py
+++ b/solution.py
@@ -49,12 +49,16 @@
 
 def block_kernel(
     n_space,
+    vol_in,
+    weights_in,
+    up_in,
+    pooled,
+    grad_out,
+    total_out,
     vol,
     weights,
     up,
-    pooled,
-    grad_out,
-    total_out,
+    load,
     rim,
     spread,
     stage,
@@ -119,6 +123,12 @@
         sent.append(copy)
         return copy
 
+    loads = [
+        pltpu.make_async_copy(source, target, load.at[i])
+        for i, (source, target) in enumerate(((vol_in, vol), (weights_in, weights), (up_in, up)))
+    ]
+    for copy in loads:
+        copy.start()
     barrier = pltpu.get_barrier_semaphore()
     for k in range(1, 8):
         pl.semaphore_signal(barrier, inc=1, device_id={"chan": along(k)}, device_id_type=MESH)
@@ -143,6 +153,8 @@
     def rows_of(plane):
         return jnp.dot(pick_rows, plane.reshape(128, 128), preferred_element_type=f32)
 
+    for copy in loads:
+        copy.wait()
     planes = [None] + [rows_of(vol[:, p]).astype(bf16) for p in range(4)]
     w = weights[...]
 
@@ -239,8 +251,6 @@
             gy[h, k].wait_recv()
         for k in range(8):
             gz[h, k].wait_recv()
-        if h == 0:
-            first_plane = send(panel.at[0], rim_panel, s_rim.at[1], r_rim.at[1], space=ahead(n_space - 1))
         grads[h] = panel[h].reshape(128, 512)
         term = lax.dot_general(taps[h], grads[h], across, preferred_element_type=f32)
         total = term if total is None else total + term
@@ -249,6 +259,10 @@
     for m in (3, 4, 5, 2, 6, 1, 7):
         peer = layer * 8 + beside(m)
         rs.append(send(terms.at[beside(m)], got.at[m], s_rs.at[m], r_rs.at[m], space=peer))
+
+    first_plane = send(
+        panel.at[0], rim_panel, s_rim.at[1], r_rim.at[1], space=ahead(n_space - 1)
+    )
 
     for z in range(2):
         for q in range(4):
@@ -364,9 +378,13 @@
             shaped(8, 4, 16, 128, dtype=bf16),
             shaped(27, 8, 128),
         ),
-        in_specs=in_vmem(3),
+        in_specs=[pl.BlockSpec(memory_space=pltpu.HBM)] * 3,
         out_specs=tuple(in_vmem(3)),
         scratch_shapes=[
+            pltpu.VMEM((8, 4, 16, 128), bf16),
+            pltpu.VMEM((216, 128), bf16),
+            pltpu.VMEM((8, 1, 4, 32), bf16),
+            dma((3,)),
             pltpu.VMEM((8, 16, 128), bf16),
             pltpu.VMEM((8, 1024), f32),
             pltpu.VMEM((3, 9, 4, 8, 128), f32),
@@ -388,7 +406,9 @@
         + [dma((8,))] * 2
         + [dma((n // 8,))] * 2
         + [dma((8,))] * 2,
-        compiler_params=pltpu.CompilerParams(collective_id=0, has_side_effects=True),
+        compiler_params=pltpu.CompilerParams(
+            collective_id=0, has_side_effects=True, vmem_limit_bytes=24 * 1024 * 1024
+        ),
     )(vol, weights, up)
 
 
@@ -403,12 +423,16 @@
         out_shape=tuple(jax.ShapeDtypeStruct(x.shape, x.dtype) for x in arrays),
         in_specs=in_vmem(3),
         out_specs=tuple(in_vmem(3)),
+        compiler_params=pltpu.CompilerParams(vmem_limit_bytes=8 * 1024 * 1024),
     )(*arrays)
 
 
 def on_device(volume, kernel, upstream):
     weights = kernel.transpose(1, 2, 3, 0, 4).reshape(216, 128)
-    pooled, input_grad, total = hand_over(*block(volume, weights, upstream))
+    held = [
+        pltpu.with_memory_space_constraint(x, pltpu.HBM) for x in (volume, weights, upstream)
+    ]
+    pooled, input_grad, total = hand_over(*block(*held))
     kernel_grad = total.reshape(3, 3, 3, 8, 128).transpose(3, 0, 1, 2, 4)
     return pooled, input_grad, kernel_grad
 

time: 54.1 us -> 51.4 us (0.950)
  Pallas kernels: 53.3 us -> 50.6 us
    pallas_call x1, Pallas kernels: 51.6 us -> 49.9 us  [block(): pl.pallas_call(lambda *refs: block_kernel(n, *refs), name='block', out_sh...]
    pallas_call x1, Pallas kernels: 1.68 us -> 0.71 us  [hand_over(): pl.pallas_call(kernel, name='hand_over', out_shape=tuple((jax.ShapeDtypeS...]
where the time goes in v6:
time: 51.4 us; the launch traced here: 51.2 us
  Pallas kernels  50.6 us (98%)
  between operations  0.64 us (1%)
    pallas_call x1, Pallas kernels, block(): pl.pallas_call(lambda *refs: block_kernel(n, *refs), name='block', out_sh...  49.9 us

profile of v6, /device:TPU:1, one launch (start us, length us, event | category | flops | bytes accessed | tf_op | source)
XLA Modules:
  0.0 51.2 jit_solution(8034905233136559017)
XLA Ops:
  0.6 49.9 %block.1 = (bf16[8,1,4,32]{3,2,1,0:T(4,128)(2,1)S(1)}, bf16[8,4,16,128]{3,2,1,0:T(8,128)(2,1)S(1)}, f32[27,8,128]{2,1,0:T(8,128)S(1)}) custom-call(bf16[8,4,16,128]{3,2,1,0:T(8,128)(2,1)} %refs_0_.1, bf16[216,128]{1,0:T(8,128)(2,1)} %bitcast.6, bf16[8,1,4,32]{3,2,1,0:T(4,128)(2,1)} %refs_2_.1), custom_call_target="tpu_custom_call" | custom-call | tf_op jit(solution)/shard_map/block/pallas_call | solution.py:373
  50.5 0.7 %hand_over.1 = (bf16[8,1,4,32]{3,2,1,0:T(4,128)(2,1)}, bf16[8,4,16,128]{3,2,1,0:T(8,128)(2,1)}, f32[27,8,128]{2,1,0:T(8,128)}) custom-call(bf16[8,1,4,32]{3,2,1,0:T(4,128)(2,1)S(1)} %get-tuple-element.9.refs_0_, bf16[8,4,16,128]{3,2,1,0:T(8,128)(2,1)S(1)} %get-tuple-element.10.refs_1_, f32[27,8,128]{2,1,0:T(8,128)S(1)} %get-tuple-element.11.refs_2_), custom_call_target="tpu_custom_call" | custom-call | tf_op jit(solution)/shard_map/hand_over/pallas_call | solution.py:420

commit v7 on v6

--- a/solution.py
+++ b/solution.py
@@ -197,6 +197,9 @@
     columns = columns_of(3)
     taps[1] = columns
     part[1] = multiply(w, columns)
+    pl.semaphore_wait(barrier, 7 + 4 + 7 + layers - 1 + 2)
+    rim_copy = send(vol.at[:, 3], rim, s_rim.at[0], r_rim.at[0], space=ahead(1))
+    send_half(1)
     stage[0:1] = jnp.zeros((1, 9, 4, 8, 128), f32)
     fill(planes[1:3], 1)
     part[0] = multiply(w, columns_of(3))
@@ -204,9 +207,6 @@
     coarse = up[...].astype(f32).reshape(8, 4, 32)
     flat = side_by_side([coarse[:, q] for q in range(4)]).astype(bf16)
     spread[...] = jnp.dot(flat, pool_picker(), preferred_element_type=f32) * 0.125
-    pl.semaphore_wait(barrier, 7 + 4 + 7 + layers - 1 + 2)
-    rim_copy = send(vol.at[:, 3], rim, s_rim.at[0], r_rim.at[0], space=ahead(1))
-    send_half(1)
     rim_copy.wait_recv()
     fill([jnp.where(space > 0, rows_of(rim[...]), 0.0).astype(bf16)], 0)
     part[0] = part[0] + multiply(w_rim, columns_of(1))
@@ -234,10 +234,11 @@
         factor = jnp.where(own[h] > 0, 1.0, slope_neg)
         panel[h, chan] = (spread[:, h * 512 : h * 512 + 512] * factor).astype(bf16)
         block = panel.at[h, chan]
-        for k in far_first:
+        for k in (4, 3, 5):
+            gz[h, k] = send(block, block, s_gz.at[h, k], r_gz.at[h, k], chan=opposite(k))
+        for k in (2, 6, 4, 3, 5, 1, 7):
             gy[h, k] = send(block, block, s_gy.at[h, k], r_gy.at[h, k], chan=along(k))
-        for k in (4, 3, 5, 0):
-            gz[h, k] = send(block, block, s_gz.at[h, k], r_gz.at[h, k], chan=opposite(k))
+        gz[h, 0] = send(block, block, s_gz.at[h, 0], r_gz.at[h, 0], chan=partner)
     for h in (1, 0):
         for k in (1, 7, 2, 6):
             gy[h, k].wait_recv()

time: 51.4 us -> 51.6 us (level)
  no operation moved by 1% of the time
where the time goes in v7:
time: 51.6 us; the launch traced here: 51.5 us
  Pallas kernels  50.9 us (99%)
  between operations  0.64 us (1%)
    pallas_call x1, Pallas kernels, block(): pl.pallas_call(lambda *refs: block_kernel(n, *refs), name='block', out_sh...  50.1 us

profile of v7, /device:TPU:1, one launch (start us, length us, event | category | flops | bytes accessed | tf_op | source)
XLA Modules:
  0.0 51.5 jit_solution(18208526021399656333)
XLA Ops:
  0.6 50.1 %block.1 = (bf16[8,1,4,32]{3,2,1,0:T(4,128)(2,1)S(1)}, bf16[8,4,16,128]{3,2,1,0:T(8,128)(2,1)S(1)}, f32[27,8,128]{2,1,0:T(8,128)S(1)}) custom-call(bf16[8,4,16,128]{3,2,1,0:T(8,128)(2,1)} %refs_0_.1, bf16[216,128]{1,0:T(8,128)(2,1)} %bitcast.6, bf16[8,1,4,32]{3,2,1,0:T(4,128)(2,1)} %refs_2_.1), custom_call_target="tpu_custom_call" | custom-call | tf_op jit(solution)/shard_map/block/pallas_call | solution.py:374
  50.8 0.7 %hand_over.1 = (bf16[8,1,4,32]{3,2,1,0:T(4,128)(2,1)}, bf16[8,4,16,128]{3,2,1,0:T(8,128)(2,1)}, f32[27,8,128]{2,1,0:T(8,128)}) custom-call(bf16[8,1,4,32]{3,2,1,0:T(4,128)(2,1)S(1)} %get-tuple-element.9.refs_0_, bf16[8,4,16,128]{3,2,1,0:T(8,128)(2,1)S(1)} %get-tuple-element.10.refs_1_, f32[27,8,128]{2,1,0:T(8,128)S(1)} %get-tuple-element.11.refs_2_), custom_call_target="tpu_custom_call" | custom-call | tf_op jit(solution)/shard_map/hand_over/pallas_call | solution.py:421

commit v8 on v7

--- a/solution.py
+++ b/solution.py
@@ -270,19 +270,6 @@
             folds[z * 4 + q] = jnp.dot(
                 w, grads[z][:, q * 128 : q * 128 + 128], preferred_element_type=f32
             ).reshape(27, 8, 128)
-    pre = side_by_side([own[0], own[1]])
-    act = jnp.where(pre > 0, pre, slope_neg * pre)
-    first = act.astype(bf16)
-    rest = act - first.astype(f32)
-    second = rest.astype(bf16)
-    third = (rest - second.astype(f32)).astype(bf16)
-    pick = pool_picker()
-    mean = sum(
-        lax.dot_general(piece, pick, across, preferred_element_type=f32)
-        for piece in (third, second, first)
-    )
-    mean = jnp.stack([mean[:, q * 32 : q * 32 + 32] for q in range(4)], axis=1)
-    pooled[...] = (mean * 0.125).astype(bf16).reshape(8, 1, 4, 32)
     share = terms[slot]
     for copy in rs:
         copy.wait_recv()
@@ -328,6 +315,19 @@
     for m in (3, 4, 5, 2, 6, 1, 7):
         block = mine.at[slot]
         ag.append(send(block, block, s_ag.at[m], r_ag.at[m], space=layer * 8 + beside(m)))
+    pre = side_by_side([own[0], own[1]])
+    act = jnp.where(pre > 0, pre, slope_neg * pre)
+    first = act.astype(bf16)
+    rest = act - first.astype(f32)
+    second = rest.astype(bf16)
+    third = (rest - second.astype(f32)).astype(bf16)
+    pick = pool_picker()
+    mean = sum(
+        lax.dot_general(piece, pick, across, preferred_element_type=f32)
+        for piece in (third, second, first)
+    )
+    mean = jnp.stack([mean[:, q * 32 : q * 32 + 32] for q in range(4)], axis=1)
+    pooled[...] = (mean * 0.125).astype(bf16).reshape(8, 1, 4, 32)
     fold = fold.reshape(3, 3, 2, 4, 8, 256)
     order = channel_first()
     depth_terms = (((1, 0),), ((2, 0), (0, 0)), ((1, 1),), ((2, 1), (0, 1)))

time: 51.6 us -> 51.7 us (level)
  no operation moved by 1% of the time
where the time goes in v8:
time: 51.7 us; the launch traced here: 51.6 us
  Pallas kernels  51 us (99%)
  between operations  0.64 us (1%)
    pallas_call x1, Pallas kernels, block(): pl.pallas_call(lambda *refs: block_kernel(n, *refs), name='block', out_sh...  50.3 us

profile of v8, /device:TPU:1, one launch (start us, length us, event | category | flops | bytes accessed | tf_op | source)
XLA Modules:
  0.0 51.6 jit_solution(11043058773881015538)
XLA Ops:
  0.6 50.3 %block.1 = (bf16[8,1,4,32]{3,2,1,0:T(4,128)(2,1)S(1)}, bf16[8,4,16,128]{3,2,1,0:T(8,128)(2,1)S(1)}, f32[27,8,128]{2,1,0:T(8,128)S(1)}) custom-call(bf16[8,4,16,128]{3,2,1,0:T(8,128)(2,1)} %refs_0_.1, bf16[216,128]{1,0:T(8,128)(2,1)} %bitcast.6, bf16[8,1,4,32]{3,2,1,0:T(4,128)(2,1)} %refs_2_.1), custom_call_target="tpu_custom_call" | custom-call | tf_op jit(solution)/shard_map/block/pallas_call | solution.py:374
  50.9 0.7 %hand_over.1 = (bf16[8,1,4,32]{3,2,1,0:T(4,128)(2,1)}, bf16[8,4,16,128]{3,2,1,0:T(8,128)(2,1)}, f32[27,8,128]{2,1,0:T(8,128)}) custom-call(bf16[8,1,4,32]{3,2,1,0:T(4,128)(2,1)S(1)} %get-tuple-element.9.refs_0_, bf16[8,4,16,128]{3,2,1,0:T(8,128)(2,1)S(1)} %get-tuple-element.10.refs_1_, f32[27,8,128]{2,1,0:T(8,128)S(1)} %get-tuple-element.11.refs_2_), custom_call_target="tpu_custom_call" | custom-call | tf_op jit(solution)/shard_map/hand_over/pallas_call | solution.py:421
